TPU v7x, 512 devices: a whole 4x8x8 slice. The times are simulated.
512 devices in a mesh: wide: 64 (over y_hi, z, x), narrow: 8 (over y_lo, core).
Axes of the slice: x: 4, y: 8 (y_hi: 2, y_lo: 4; y = y_hi * 4 + y_lo), z: 8, core: 2. Of those that a mesh axis runs over, the one named last changes fastest.
Arguments:
- wavefunction: float32 [33554432], P(('wide', 'narrow')), may hold values from -6 to 6
- propagator: float32 [705432], replicated, may hold values from -2.5 to 3.5, as said below
- gate_orders: int32 [6, 11], replicated, may hold values from 0 to 10, each once within a row
- sector_order: int32 [2048], replicated, may hold values from 0 to 2047, as said below
- bond_level: int32 [24], replicated, may hold values from -3 to 3
Outputs:
- evolved: float32 [33554432], P(('wide', 'narrow'))
Inputs may be any that keep to these rules, and one draw needn't show every extreme that they name: `propagator`: sector blocks for k = 0 .. 11 set bits, each row-major, one after another in increasing k. `sector_order`: a permutation of 0 .. 2047 listing states with fewer set bits first.
All inputs are finite; a program needn't handle non-finite values.
Results may differ from a plain program's by a relative error of at most 0.0001.
Values sent between devices are 32-bit elements; how exact they have to be, the bound alone decides.
No kernel may reach another device: no remote copies, remote signals or barrier semaphores. Data moves between devices by JAX's collectives and lax.ppermute only.
A program may use at most 64 MiB of HBM per device.

v0:
```python
import math

import jax
import jax.numpy as jnp
from jax import lax
from jax.experimental import pallas as pl
from jax.experimental.pallas import tpu as pltpu
from jax.sharding import PartitionSpec as P

LB = 16
GS = 11
STATES = 2048
ZZ_RATE = 0.06
F32 = jnp.float32
BF16 = jnp.bfloat16

SIZES = [math.comb(GS, k) for k in range(GS + 1)]
PROP_ROWS = 5512
GROUPS = [
    (0, 232, 0, 256, 0, 240),
    (232, 330, 256, 384, 240, 336),
    (562, 462, 640, 512, 576, 464),
    (1024, 462, 1152, 512, 1040, 464),
    (1486, 330, 1664, 384, 1504, 336),
    (1816, 232, 2048, 256, 1840, 240),
]
U_ROWS = 2304
B_ROWS = 2080
UNROLL = 16


def lay_out_blocks(flat, blocks):
    starts = []
    at = 0
    for n in SIZES:
        starts.append(at)
        at += n * n
    lane = lax.broadcasted_iota(jnp.int32, (8, 128), 1)

    def shifted(piece_of, count, shift, columns):
        pieces = []
        for i in range(columns + (1 if shift else 0)):
            piece = piece_of(i)
            pieces.append(pltpu.roll(piece, 128 - shift, 1) if shift else piece)
        if not shift:
            return pieces
        keep = lane[:count] < 128 - shift
        return [jnp.where(keep, pieces[i], pieces[i + 1]) for i in range(columns)]

    for degree, group in ((4, 1), (5, 2), (6, 3), (7, 4)):
        n = SIZES[degree]
        row0 = GROUPS[group][4]
        columns = -(-n // 128)
        step = n // 2
        for s in range(64):
            count = len(range(s, n, 64))
            first, shift = divmod(starts[degree] + n * s, 128)
            rows = shifted(
                lambda i: flat[pl.ds(first + i, count, stride=step), :], count, shift, columns
            )
            for i in range(columns):
                blocks[pl.ds(i * B_ROWS + row0 + s, count, stride=64), :] = rows[i]
    for group, degrees in ((0, (0, 1, 2, 3)), (5, (8, 9, 10, 11))):
        row0 = GROUPS[group][4]
        column = 0
        for degree in degrees:
            n = SIZES[degree]
            for r in range(n):
                origin = starts[degree] + n * r - column
                first, shift = divmod(origin, 128)
                for i in range(2):
                    low, high = max(column, 128 * i), min(column + n, 128 * i + 128)
                    if low >= high:
                        blocks[pl.ds(i * B_ROWS + row0 + column + r, 1), :] = jnp.zeros((1, 128), F32)
                        continue
                    low, high = low - 128 * i, high - 128 * i
                    value = None
                    if low < 128 - shift:
                        value = flat[pl.ds(first + i, 1), :]
                        if shift:
                            value = pltpu.roll(value, 128 - shift, 1)
                    if shift and high > 128 - shift:
                        after = pltpu.roll(flat[pl.ds(first + i + 1, 1), :], 128 - shift, 1)
                        value = (
                            after
                            if value is None
                            else jnp.where(lane[:1] < 128 - shift, value, after)
                        )
                    if low > 0 or high < 128:
                        value = jnp.where((lane[:1] >= low) & (lane[:1] < high), value, 0.0)
                    blocks[pl.ds(i * B_ROWS + row0 + column + r, 1), :] = value
            column += n


def split_blocks(blocks, hi, lo):
    def body(t, carry):
        at = pl.multiple_of(t * 16, 16)
        rows = pl.ds(at, 16)
        for i in range(4):
            x = blocks[pl.ds(i * B_ROWS + at, 16), :]
            h = x.astype(BF16)
            hi[rows, i * 128 : (i + 1) * 128] = h
            lo[rows, i * 128 : (i + 1) * 128] = (x - h.astype(F32)).astype(BF16)
        return carry

    lax.fori_loop(0, B_ROWS // 16, body, 0)


def clear_pads(u):
    for _, n, at, rows, _, _ in GROUPS:
        u[pl.ds(at + n, rows - n), :] = jnp.zeros((rows - n, 128), F32)


def over_rows(move):
    for number, (first, n, _, _, _, _) in enumerate(GROUPS):

        def body(t, carry):
            base = pl.multiple_of(t * UNROLL, UNROLL)
            for i in range(UNROLL):
                move(number, first + base + i, base + i)
            return carry

        whole = n // UNROLL
        lax.fori_loop(0, whole, body, 0)
        for r in range(whole * UNROLL, n):
            move(number, first + r, r)


def gather(source, u, table, offset):
    def move(number, j, r):
        u[pl.ds(GROUPS[number][2] + r, 1), :] = source[pl.ds(table[offset + j], 1), :]

    over_rows(move)


def scatter(y, target, table, offset):
    def move(number, j, r):
        target[pl.ds(table[offset + j], 1), :] = y[pl.ds(GROUPS[number][4] + r, 1), :]

    over_rows(move)


def scatter_lanes(y, target, table, offset):
    group_of_lane = lax.shift_right_logical(lax.broadcasted_iota(jnp.int32, (1, 128), 1), 5)

    def move(number, j, r):
        code = table[offset + j]
        row = lax.shift_right_logical(code, 2)
        pltpu.store(
            target.at[pl.ds(row, 1), :],
            y[pl.ds(GROUPS[number][4] + r, 1), :],
            mask=group_of_lane == (code & 3),
        )

    over_rows(move)


def multiply(u, y, hi, lo):
    for _, _, u_at, k, b_at, m in GROUPS:
        x = u[pl.ds(u_at, k), :]
        xh = x.astype(BF16)
        xl = (x - xh.astype(F32)).astype(BF16)
        h = hi[pl.ds(b_at, m), :k]
        both = jnp.dot(h, jnp.concatenate([xh, xl], axis=1), preferred_element_type=F32)
        rest = jnp.dot(lo[pl.ds(b_at, m), :k], xh, preferred_element_type=F32)
        y[pl.ds(b_at, m), :] = both[:, :128] + both[:, 128:] + rest


def spread(value, source, at):
    rows = value.shape[0]
    group_of_lane = lax.shift_right_logical(lax.broadcasted_iota(jnp.int32, (rows, 128), 1), 5)
    turned = [value] + [pltpu.roll(value, 32 * t, 1) for t in (1, 2, 3)]
    for g in range(4):
        out = turned[(0 - g) % 4]
        for t in (1, 2, 3):
            out = jnp.where(group_of_lane == t, turned[(t - g) % 4], out)
        source[pl.ds(512 * g + at, rows), :] = out


def spread_all(values, source):
    def body(t, carry):
        at = pl.multiple_of(t * 32, 32)
        spread(values(at, 32), source, at)
        return carry

    lax.fori_loop(0, 16, body, 0)


def turn_in(block, source, g):
    source[pl.ds(128 * g, 128), :] = jnp.concatenate([block] * 4, axis=0).T


def turn_all(folded, source):
    for g in range(16):
        turn_in(folded[pl.ds(32 * g, 32), :], source, g)


def turn_out(source, out):
    for g in range(16):
        out[pl.ds(g, 32, stride=16), :] = source[pl.ds(128 * g, 128), :].T[:32]


def spin(index, position):
    return 1 - 2 * (lax.shift_right_logical(index, position) & 1)


def first_kernel(table, levels, wave, flat, out, hi, lo, blocks, u, y, source, folded):
    device = lax.axis_index("wide") * 8 + lax.axis_index("narrow")
    high = jnp.int32(0)
    for s in range(8):
        high = high + levels[LB + s] * spin(device, s) * spin(device, s + 1)
    border = levels[LB - 1] * spin(device, 0)
    lane = lax.broadcasted_iota(jnp.int32, (32, 128), 1)
    lane_energy = jnp.zeros((32, 128), jnp.int32) + high
    for s in range(6):
        lane_energy = lane_energy + levels[s] * (spin(lane, s) * spin(lane, s + 1))
    last_lane_spin = spin(lane, 6)

    def phased(at, rows):
        row = lax.broadcasted_iota(jnp.int32, (32, 128), 0) + at
        spins = [spin(row, s) for s in range(9)]
        energy = lane_energy + levels[6] * (last_lane_spin * spins[0]) + border * spins[8]
        for s in range(8):
            energy = energy + levels[7 + s] * (spins[s] * spins[s + 1])
        return wave[pl.ds(at, rows), :] * jnp.exp(-ZZ_RATE * energy.astype(F32))

    lay_out_blocks(flat, blocks)
    split_blocks(blocks, hi, lo)
    clear_pads(u)
    spread_all(phased, source)
    gather(source, u, table, 0)
    multiply(u, y, hi, lo)
    scatter_lanes(y, folded, table, STATES)
    turn_all(folded, source)
    gather(source, u, table, 2 * STATES)
    multiply(u, y, hi, lo)
    scatter(y, source, table, 3 * STATES)
    turn_out(source, out)


def second_kernel(table, amplitudes, hi, lo, out, u, y, source):
    clear_pads(u)
    spread_all(lambda at, rows: amplitudes[pl.ds(at, rows), :], source)
    gather(source, u, table, 0)
    multiply(u, y, hi, lo)
    scatter_lanes(y, out, table, STATES)


def third_kernel(table, amplitudes, hi, lo, out, u, y, source, folded):
    clear_pads(u)
    for g in range(16):
        turn_in(amplitudes[pl.ds(g, 32, stride=16), :], source, g)
    gather(source, u, table, 0)
    multiply(u, y, hi, lo)
    scatter_lanes(y, folded, table, STATES)
    turn_all(folded, source)
    gather(source, u, table, 2 * STATES)
    multiply(u, y, hi, lo)
    scatter_lanes(y, folded, table, 3 * STATES)
    turn_all(folded, source)
    gather(source, u, table, 4 * STATES)
    multiply(u, y, hi, lo)
    scatter(y, source, table, 5 * STATES)
    turn_out(source, out)


SMEM = pl.BlockSpec(memory_space=pltpu.SMEM)
VMEM = pl.BlockSpec(memory_space=pltpu.VMEM)
AMPLITUDES = jax.ShapeDtypeStruct((512, 128), F32)
BLOCKS = jax.ShapeDtypeStruct((B_ROWS, 512), BF16)
U = pltpu.VMEM((U_ROWS, 128), F32)
Y = pltpu.VMEM((B_ROWS, 128), F32)
SOURCE = pltpu.VMEM((STATES, 128), F32)
FOLDED = pltpu.VMEM((512, 128), F32)


def index_tables(gate_orders, sector_order):
    mapped = jnp.zeros((gate_orders.shape[0], STATES), jnp.int32)
    for position in range(GS):
        chosen = jnp.right_shift(sector_order, position) & 1
        mapped = mapped + jnp.left_shift(chosen[None, :], gate_orders[:, position : position + 1])
    c0, c1, c2, c3, c4, c5 = (mapped[g] for g in range(6))

    def quarters(c):
        return (c & 3) * 512 + (c >> 2)

    def fold_top(c):
        mid = c & 63
        return ((mid >> 2) * 32 + (c >> 6)) * 4 + (mid & 3)

    def fold_low(c):
        mid = c >> 5
        return ((mid >> 2) * 32 + (c & 31)) * 4 + (mid & 3)

    first = jnp.concatenate([quarters(c0), fold_top(c0), c1, c1])
    second = jnp.concatenate([quarters(c2), c2])
    third = jnp.concatenate(
        [c3, fold_low(c3), (c4 & 63) * 32 + (c4 >> 6), fold_top(c4), c5, c5]
    )
    return first, second, third


def exchange(amplitudes):
    return lax.all_to_all(amplitudes, ("narrow", "wide"), split_axis=0, concat_axis=0, tiled=True)


def shards(wavefunction, propagator, gate_orders, sector_order, bond_level):
    first, second, third = index_tables(gate_orders, sector_order)
    flat = jnp.pad(propagator, (0, PROP_ROWS * 128 - propagator.shape[0])).reshape(-1, 128)
    amplitudes, hi, lo = pl.pallas_call(
        first_kernel,
        out_shape=(AMPLITUDES, BLOCKS, BLOCKS),
        in_specs=[SMEM, SMEM, VMEM, VMEM],
        out_specs=(VMEM, VMEM, VMEM),
        scratch_shapes=[pltpu.VMEM((4 * B_ROWS, 128), F32), U, Y, SOURCE, FOLDED],
        name="first",
    )(first, bond_level, wavefunction.reshape(512, 128), flat)
    amplitudes = exchange(amplitudes)
    amplitudes = pl.pallas_call(
        second_kernel,
        out_shape=AMPLITUDES,
        in_specs=[SMEM, VMEM, VMEM, VMEM],
        out_specs=VMEM,
        scratch_shapes=[U, Y, SOURCE],
        name="second",
    )(second, amplitudes, hi, lo)
    amplitudes = exchange(amplitudes)
    amplitudes = pl.pallas_call(
        third_kernel,
        out_shape=AMPLITUDES,
        in_specs=[SMEM, VMEM, VMEM, VMEM],
        out_specs=VMEM,
        scratch_shapes=[U, Y, SOURCE, FOLDED],
        name="third",
    )(third, amplitudes, hi, lo)
    return amplitudes.reshape(-1)


def solution(mesh):
    in_specs = (P(("wide", "narrow")), P(), P(), P(), P())
    out_specs = P(("wide", "narrow"))
    return jax.shard_map(shards, mesh=mesh, in_specs=in_specs, out_specs=out_specs, check_vma=False)
```

profile of v0, /device:TPU:1, one launch (start us, length us, event | category | flops | bytes accessed | tf_op | source)
XLA Modules:
  0.0 131.7 jit_solution(4337421062626873865)
XLA Ops:
  0.0 0.7 shift-right-arithmetic_and_fusion.10
  0.7 1.5 %slice_reduce_fusion.10 = (s32[6]{0:T(128)S(1)}, s32[6]{0:T(128)S(1)}, s32[6]{0:T(128)S(1)}, s32[6]{0:T(128)S(1)}, s32[6]{0:T(128)S(1)}, /*index=5*/s32[6]{0:T(1...) fusion(s32[6,11]{1,0:T(8,128)} %param.7), kind=kLoop, calls=%fused_computation.38 | loop fusion | bytes 528 | tf_op jit(solution)/shard_map/slice | solution.py:281
  2.2 0.1 shift-left_add_fusion
  2.3 0.1 shift-right-arithmetic_add_fusion
  2.4 3.6 %pad_bitcast_fusion.flat = f32[5512,128]{1,0:T(8,128)} fusion(f32[705432]{0:T(1024)} %param.6), kind=kLoop, calls=%fused_computation | loop fusion | bytes 5643872 | tf_op jit(solution)/shard_map/reshape | solution.py:309
  5.9 0.6 pad_add_fusion.table
  6.5 24.2 %first.1 = (f32[512,128]{1,0:T(8,128)}, bf16[2080,512]{1,0:T(8,128)(2,1)}, bf16[2080,512]{1,0:T(8,128)(2,1)}) custom-call(s32[8192]{0:T(1024)} %pad_add_fusion.table, s32[24]{0:T(128)} %levels.1, f32[512,128]{1,0:T(8,128)} %bitcast.23, f32[5512,128]{1,0:T(8,128)} %pad_bitcast_fusion.flat), custom_call_target="tpu_custom_call" | custom-call | tf_op jit(solution)/shard_map/first/pallas_call | solution.py:310
  30.8 22.1 %all-to-all-start = ((f32[512,1,128]{2,1,0:T(1,128)}), f32[512,1,128]{2,1,0:T(1,128)S(1)}, u32[]{:S(2)}, u32[]{:S(2)}) async-start(f32[512,1,128]{2,1,0:T(1,128)} %bitcast.24), calls=%async_computation | async-start | bytes 524288 | tf_op jit(solution)/shard_map/all_to_all | solution.py:304
  52.9 0.6 pad_add_fusion.1.table
  53.5 16.5 %all-to-all-done = f32[512,1,128]{2,1,0:T(1,128)S(1)} async-done(((f32[512,1,128]{2,1,0:T(1,128)}), f32[512,1,128]{2,1,0:T(1,128)S(1)}, u32[]{:S(2)}, u32[]{:S(2)}) %all-to-all-start) | async-done | bytes 262176 | tf_op jit(solution)/shard_map/all_to_all | solution.py:304
  70.1 0.0 copy-start.1
  70.1 0.7 copy-done.1
  70.8 11.1 %second.1 = f32[512,128]{1,0:T(8,128)} custom-call(s32[4096]{0:T(1024)} %pad_add_fusion.1.table, f32[512,128]{1,0:T(8,128)} %bitcast.22, bf16[2080,512]{1,0:T(8,128)(2,1)} %get-tuple-element.9.hi, bf16[2080,512]{1,0:T(8,128)(2,1)} %get-tuple-element.10.lo), custom_call_target="tpu_custom_call" | custom-call | tf_op jit(solution)/shard_map/second/pallas_call | solution.py:319
  81.8 8.5 %all-to-all-start.1 = ((f32[512,1,128]{2,1,0:T(1,128)}), f32[512,1,128]{2,1,0:T(1,128)S(1)}, u32[]{:S(2)}, u32[]{:S(2)}) async-start(f32[512,1,128]{2,1,0:T(1,128)} %bitcast.21), calls=%async_computation.1 | async-start | bytes 524288 | tf_op jit(solution)/shard_map/all_to_all | solution.py:304
  90.4 0.0 copy-start.2
  90.4 17.3 %all-to-all-done.1 = f32[512,1,128]{2,1,0:T(1,128)S(1)} async-done(((f32[512,1,128]{2,1,0:T(1,128)}), f32[512,1,128]{2,1,0:T(1,128)S(1)}, u32[]{:S(2)}, u32[]{:S(2)}) %all-to-all-start.1) | async-done | bytes 262176 | tf_op jit(solution)/shard_map/all_to_all | solution.py:304
  107.7 0.0 copy-start
  107.7 0.0 copy-done.2
  107.7 0.7 copy-done
  108.4 23.3 %third.1 = f32[512,128]{1,0:T(8,128)} custom-call(s32[12288]{0:T(1024)} %copy-done.2, f32[512,128]{1,0:T(8,128)} %bitcast.20, bf16[2080,512]{1,0:T(8,128)(2,1)} %get-tuple-element.9.hi, bf16[2080,512]{1,0:T(8,128)(2,1)} %get-tuple-element.10.lo), custom_call_target="tpu_custom_call" | custom-call | tf_op jit(solution)/shard_map/third/pallas_call | solution.py:328
  (7 shorter events, 0.0 us)
Async XLA Ops:
  30.8 39.3 %all-to-all-start = ((f32[512,1,128]{2,1,0:T(1,128)}), f32[512,1,128]{2,1,0:T(1,128)S(1)}, u32[]{:S(2)}, u32[]{:S(2)}) async-start(f32[512,1,128]{2,1,0:T(1,128)} %bitcast.24), calls=%async_computation | async-start | bytes 524288 | tf_op jit(solution)/shard_map/all_to_all | solution.py:304
  70.1 0.7 copy-start.1
  81.8 25.9 %all-to-all-start.1 = ((f32[512,1,128]{2,1,0:T(1,128)}), f32[512,1,128]{2,1,0:T(1,128)S(1)}, u32[]{:S(2)}, u32[]{:S(2)}) async-start(f32[512,1,128]{2,1,0:T(1,128)} %bitcast.21), calls=%async_computation.1 | async-start | bytes 524288 | tf_op jit(solution)/shard_map/all_to_all | solution.py:304
  90.4 17.3 %copy-start.2 = (s32[12288]{0:T(1024)}, s32[12288]{0:T(1024)S(1)}, u32[]{:S(2)}) copy-start(s32[12288]{0:T(1024)S(1)} %constant_dynamic-update-slice_fusion.table) | copy-start | bytes 147460
  107.7 0.7 copy-start
where the time goes:
time: 132 us
  Pallas kernels  58.6 us (44%)
  waiting for transfers between devices  33.8 us (26%)
  starting transfers between devices  30.7 us (23%)
  local copies, waits for them, and re-layouts  6.42 us (5%)
  other arithmetic  2.13 us (2%)
    all_to_all x2, waiting for transfers between devices, exchange(): lax.all_to_all(amplitudes, ('narrow', 'wide'), split_axis=0, concat_axis=...  33.8 us
    all_to_all x2, starting transfers between devices, exchange(): lax.all_to_all(amplitudes, ('narrow', 'wide'), split_axis=0, concat_axis=...  30.7 us
    pallas_call x1, Pallas kernels, shards(): pl.pallas_call(first_kernel, out_shape=(AMPLITUDES, BLOCKS, BLOCKS), in_s...  24.2 us
    pallas_call x1, Pallas kernels, shards(): pl.pallas_call(third_kernel, out_shape=AMPLITUDES, in_specs=[SMEM, VMEM,...  23.3 us
    pallas_call x1, Pallas kernels, shards(): pl.pallas_call(second_kernel, out_shape=AMPLITUDES, in_specs=[SMEM, VMEM,...  11.1 us
    reshape x1, local copies, waits for them, and re-layouts, shards(): jnp.pad(propagator, (0, PROP_ROWS * 128 - propagator.shape[0]))  3.56 us
  transfers between devices with their start and end apart: 2, of which 2 were waited for; matrix products, arithmetic and copies ran while one was open for 0% of the time, Pallas kernels for 0%

commit v1 on v0

v1 whole, which is shorter than its diff:
```python
import math

import jax
import jax.numpy as jnp
from jax import lax
from jax.experimental import pallas as pl
from jax.experimental.pallas import tpu as pltpu
from jax.sharding import PartitionSpec as P

LB = 16
GS = 11
STATES = 2048
ZZ_RATE = 0.06
F32 = jnp.float32
BF16 = jnp.bfloat16

SIZES = [math.comb(GS, k) for k in range(GS + 1)]
PROP_ROWS = 5512
NT = (((1,), (1,)), ((), ()))
GROUPS = [
    (0, 232, 0, 256),
    (232, 330, 256, 384),
    (562, 462, 640, 512),
    (1024, 462, 1152, 512),
    (1486, 330, 1664, 384),
    (1816, 232, 2048, 256),
]
PADDED = 2304
PADDED_BLOCKS = PADDED // 128
BLOCKS = STATES // 128


def lay_out_blocks(flat, blocks):
    starts = []
    at = 0
    for n in SIZES:
        starts.append(at)
        at += n * n
    lane = lax.broadcasted_iota(jnp.int32, (8, 128), 1)

    def shifted(piece_of, count, shift, columns):
        pieces = []
        for i in range(columns + (1 if shift else 0)):
            piece = piece_of(i)
            pieces.append(pltpu.roll(piece, 128 - shift, 1) if shift else piece)
        if not shift:
            return pieces
        keep = lane[:count] < 128 - shift
        return [jnp.where(keep, pieces[i], pieces[i + 1]) for i in range(columns)]

    for degree, group in ((4, 1), (5, 2), (6, 3), (7, 4)):
        n = SIZES[degree]
        row0 = GROUPS[group][2]
        columns = -(-n // 128)
        step = n // 2
        for s in range(64):
            count = len(range(s, n, 64))
            first, shift = divmod(starts[degree] + n * s, 128)
            rows = shifted(
                lambda i: flat[pl.ds(first + i, count, stride=step), :], count, shift, columns
            )
            for i in range(columns):
                blocks[pl.ds(i * PADDED + row0 + s, count, stride=64), :] = rows[i]
    for group, degrees in ((0, (0, 1, 2, 3)), (5, (8, 9, 10, 11))):
        row0 = GROUPS[group][2]
        column = 0
        for degree in degrees:
            n = SIZES[degree]
            for r in range(n):
                origin = starts[degree] + n * r - column
                first, shift = divmod(origin, 128)
                for i in range(2):
                    low, high = max(column, 128 * i), min(column + n, 128 * i + 128)
                    if low >= high:
                        blocks[pl.ds(i * PADDED + row0 + column + r, 1), :] = jnp.zeros((1, 128), F32)
                        continue
                    low, high = low - 128 * i, high - 128 * i
                    value = None
                    if low < 128 - shift:
                        value = flat[pl.ds(first + i, 1), :]
                        if shift:
                            value = pltpu.roll(value, 128 - shift, 1)
                    if shift and high > 128 - shift:
                        after = pltpu.roll(flat[pl.ds(first + i + 1, 1), :], 128 - shift, 1)
                        value = (
                            after
                            if value is None
                            else jnp.where(lane[:1] < 128 - shift, value, after)
                        )
                    if low > 0 or high < 128:
                        value = jnp.where((lane[:1] >= low) & (lane[:1] < high), value, 0.0)
                    blocks[pl.ds(i * PADDED + row0 + column + r, 1), :] = value
            column += n


def split_blocks(blocks, hi, lo):
    def body(t, carry):
        at = pl.multiple_of(t * 16, 16)
        rows = pl.ds(at, 16)
        for i in range(4):
            x = blocks[pl.ds(i * PADDED + at, 16), :]
            h = x.astype(BF16)
            hi[rows, i * 128 : (i + 1) * 128] = h
            lo[rows, i * 128 : (i + 1) * 128] = (x - h.astype(F32)).astype(BF16)
        return carry

    lax.fori_loop(0, PADDED // 16, body, 0)


def pad_order(order, padded):
    lane = lax.broadcasted_iota(jnp.int32, (1, 128), 1)
    for first, n, at, rows in GROUPS:
        for r in range(0, rows, 128):
            block, shift = divmod(first + r, 128)
            value = order[pl.ds(min(block, BLOCKS - 1), 1), :]
            if shift:
                after = order[pl.ds(min(block + 1, BLOCKS - 1), 1), :]
                value = jnp.where(
                    lane < 128 - shift,
                    pltpu.roll(value, 128 - shift, 1),
                    pltpu.roll(after, 128 - shift, 1),
                )
            if r + 128 > n:
                value = jnp.where(lane < n - r, value, -1)
            padded[pl.ds((at + r) // 128, 1), :] = value
    spare = 24 - PADDED_BLOCKS
    padded[pl.ds(PADDED_BLOCKS, spare), :] = jnp.full((spare, 128), -1, jnp.int32)


def invert_order(padded, places):
    total = jnp.zeros((32, 128), F32)
    lane = lax.broadcasted_iota(jnp.int32, (16, 128), 1)
    row = lax.broadcasted_iota(jnp.int32, (16, 128), 0)
    column = lax.broadcasted_iota(jnp.int32, (128, 128), 0)
    for o in range(PADDED_BLOCKS):
        state = padded[pl.ds(o, 1), :]
        place = lane + 128 * o
        hit = lax.shift_right_arithmetic(state, 7) == row
        left = jnp.concatenate(
            [
                jnp.where(hit, lax.shift_right_logical(place, 4).astype(F32), 0.0),
                jnp.where(hit, (place & 15).astype(F32), 0.0),
            ],
            axis=0,
        ).astype(BF16)
        right = jnp.where((state & 127) == column, 1.0, 0.0).astype(BF16)
        total = total + lax.dot_general(left, right, NT, preferred_element_type=F32)
    places[...] = (16.0 * total[:16] + total[16:]).astype(jnp.int32)


def take(row, index):
    return jnp.take_along_axis(row, index, axis=1, mode="promise_in_bounds")


def tables(orders, gate, top, padded, places, pull, push):
    state = padded[...]
    mapped = jnp.zeros_like(state)
    for t in range(GS):
        mapped = mapped + lax.shift_left(
            lax.shift_right_logical(state, t) & 1, jnp.full_like(state, orders[gate, t])
        )
    if top:
        mapped = (mapped & 3) * 512 + lax.shift_right_logical(mapped, 2)
    pull[...] = jnp.where(state < 0, -1, mapped)
    for half in range(2):
        place = lax.broadcasted_iota(jnp.int32, (8, 128), 0) * 128 + lax.broadcasted_iota(
            jnp.int32, (8, 128), 1
        )
        place = place + half * 1024
        if top:
            place = (place & 511) * 4 + lax.shift_right_logical(place, 9)
        state = jnp.zeros_like(place)
        for t in range(GS):
            bit = lax.shift_right_logical(place, jnp.full_like(place, orders[gate, t])) & 1
            state = state + bit * (1 << t)
        block, lane = lax.shift_right_logical(state, 7), state & 127
        found = jnp.zeros_like(place)
        for i in range(BLOCKS):
            row = jnp.broadcast_to(places[pl.ds(i, 1), :], (8, 128))
            found = jnp.where(block == i, take(row, lane), found)
        push[pl.ds(8 * half, 8), :] = found


def permute(source, target, table, source_blocks, target_blocks, unroll):
    def body(t, carry):
        for step in range(unroll):
            o = t * unroll + step
            index = jnp.broadcast_to(table[pl.ds(o, 1), :], (8, 128))
            block, lane = lax.shift_right_arithmetic(index, 7), index & 127
            hits = [block == i for i in range(source_blocks)]
            for b in range(4):
                found = jnp.zeros((8, 128), F32)
                for i in range(source_blocks):
                    piece = source[8 * b : 8 * b + 8, 128 * i : 128 * i + 128]
                    found = jnp.where(hits[i], take(piece, lane), found)
                target[8 * b : 8 * b + 8, pl.ds(pl.multiple_of(o * 128, 128), 128)] = found
        return carry

    lax.fori_loop(0, target_blocks // unroll, body, 0)


def multiply(u, y, hi, lo):
    for _, _, at, k in GROUPS:
        x = u[:, at : at + k]
        xh = x.astype(BF16)
        xl = (x - xh.astype(F32)).astype(BF16)
        both = lax.dot_general(
            jnp.concatenate([xh, xl], axis=0),
            hi[at : at + k, :k],
            NT,
            preferred_element_type=F32,
        )
        rest = lax.dot_general(xh, lo[at : at + k, :k], NT, preferred_element_type=F32)
        y[:, at : at + k] = both[:32] + both[32:] + rest


def gate(orders, number, top, x, u, y, hi, lo, padded, places, pull, push):
    tables(orders, number, top, padded, places, pull, push)
    permute(x, u, pull, BLOCKS, PADDED_BLOCKS, 3)
    multiply(u, y, hi, lo)
    permute(y, x, push, PADDED_BLOCKS, BLOCKS, 2)


def turn_in(value, at, x):
    turned = value.T
    for g in range(4):
        x[:, 512 * g + at : 512 * g + at + 128] = turned[32 * g : 32 * g + 32]


def top_in(amplitudes, x):
    for at in range(0, 512, 128):
        turn_in(amplitudes[pl.ds(at, 128), :], at, x)


def top_out(x, out):
    for at in range(0, 512, 128):
        pieces = [x[:, 512 * g + at : 512 * g + at + 128] for g in range(4)]
        out[pl.ds(at, 128), :] = jnp.concatenate(pieces, axis=0).T


def low_in(amplitudes, x):
    for g in range(16):
        x[:, 128 * g : 128 * g + 128] = amplitudes[pl.ds(g, 32, stride=16), :]


def low_out(x, out):
    for g in range(16):
        out[pl.ds(g, 32, stride=16), :] = x[:, 128 * g : 128 * g + 128]


def spin(index, position):
    return 1 - 2 * (lax.shift_right_logical(index, position) & 1)


def first_kernel(
    orders, levels, order, wave, flat, out, hi, lo, padded, places, blocks, x, u, y, pull, push, plain
):
    device = lax.axis_index("wide") * 8 + lax.axis_index("narrow")
    high = jnp.int32(0)
    for s in range(8):
        high = high + levels[LB + s] * spin(device, s) * spin(device, s + 1)
    border = levels[LB - 1] * spin(device, 0)
    lane = lax.broadcasted_iota(jnp.int32, (128, 128), 1)
    lane_energy = jnp.zeros((128, 128), jnp.int32) + high
    for s in range(6):
        lane_energy = lane_energy + levels[s] * (spin(lane, s) * spin(lane, s + 1))
    last_lane_spin = spin(lane, 6)

    lay_out_blocks(flat, blocks)
    split_blocks(blocks, hi, lo)
    pad_order(order, padded)
    invert_order(padded, places)
    for at in range(0, 512, 128):
        row = lax.broadcasted_iota(jnp.int32, (128, 128), 0) + at
        spins = [spin(row, s) for s in range(9)]
        energy = lane_energy + levels[6] * (last_lane_spin * spins[0]) + border * spins[8]
        for s in range(8):
            energy = energy + levels[7 + s] * (spins[s] * spins[s + 1])
        turn_in(wave[pl.ds(at, 128), :] * jnp.exp(-ZZ_RATE * energy.astype(F32)), at, x)
    rest = (x, u, y, hi, lo, padded, places, pull, push)
    gate(orders, 0, True, *rest)
    top_out(x, plain)
    low_in(plain, x)
    gate(orders, 1, False, *rest)
    low_out(x, out)


def second_kernel(orders, amplitudes, hi, lo, padded, places, out, x, u, y, pull, push):
    top_in(amplitudes, x)
    gate(orders, 2, True, x, u, y, hi, lo, padded, places, pull, push)
    top_out(x, out)


def third_kernel(orders, amplitudes, hi, lo, padded, places, out, x, u, y, pull, push, plain):
    rest = (x, u, y, hi, lo, padded, places, pull, push)
    low_in(amplitudes, x)
    gate(orders, 3, False, *rest)
    low_out(x, plain)
    top_in(plain, x)
    gate(orders, 4, True, *rest)
    top_out(x, plain)
    low_in(plain, x)
    gate(orders, 5, False, *rest)
    low_out(x, out)


SMEM = pl.BlockSpec(memory_space=pltpu.SMEM)
VMEM = pl.BlockSpec(memory_space=pltpu.VMEM)
AMPLITUDES = jax.ShapeDtypeStruct((512, 128), F32)
HALVES = jax.ShapeDtypeStruct((PADDED, 512), BF16)
SCRATCH = [
    pltpu.VMEM((32, STATES), F32),
    pltpu.VMEM((32, PADDED), F32),
    pltpu.VMEM((32, PADDED), F32),
    pltpu.VMEM((24, 128), jnp.int32),
    pltpu.VMEM((16, 128), jnp.int32),
]
PLAIN = pltpu.VMEM((512, 128), F32)


def exchange(amplitudes):
    return lax.all_to_all(amplitudes, ("narrow", "wide"), split_axis=0, concat_axis=0, tiled=True)


def shards(wavefunction, propagator, gate_orders, sector_order, bond_level):
    flat = jnp.pad(propagator, (0, PROP_ROWS * 128 - propagator.shape[0])).reshape(-1, 128)
    amplitudes, *rest = pl.pallas_call(
        first_kernel,
        out_shape=(
            AMPLITUDES,
            HALVES,
            HALVES,
            jax.ShapeDtypeStruct((24, 128), jnp.int32),
            jax.ShapeDtypeStruct((16, 128), jnp.int32),
        ),
        in_specs=[SMEM, SMEM, VMEM, VMEM, VMEM],
        out_specs=(VMEM,) * 5,
        scratch_shapes=[pltpu.VMEM((4 * PADDED, 128), F32), *SCRATCH, PLAIN],
        name="first",
    )(gate_orders, bond_level, sector_order.reshape(16, 128), wavefunction.reshape(512, 128), flat)
    amplitudes = exchange(amplitudes)
    amplitudes = pl.pallas_call(
        second_kernel,
        out_shape=AMPLITUDES,
        in_specs=[SMEM] + [VMEM] * 5,
        out_specs=VMEM,
        scratch_shapes=SCRATCH,
        name="second",
    )(gate_orders, amplitudes, *rest)
    amplitudes = exchange(amplitudes)
    amplitudes = pl.pallas_call(
        third_kernel,
        out_shape=AMPLITUDES,
        in_specs=[SMEM] + [VMEM] * 5,
        out_specs=VMEM,
        scratch_shapes=[*SCRATCH, PLAIN],
        name="third",
    )(gate_orders, amplitudes, *rest)
    return amplitudes.reshape(-1)


def solution(mesh):
    in_specs = (P(("wide", "narrow")), P(), P(), P(), P())
    out_specs = P(("wide", "narrow"))
    return jax.shard_map(shards, mesh=mesh, in_specs=in_specs, out_specs=out_specs, check_vma=False)
```

time: 132 us -> 119 us (0.902)
  blocking collectives: 0 us -> 67.9 us
  waiting for transfers between devices: 33.8 us -> 0 us
  starting transfers between devices: 30.7 us -> 0 us
  Pallas kernels: 58.6 us -> 47.2 us
  local copies, waits for them, and re-layouts: 6.42 us -> 3.57 us
  other arithmetic: 2.13 us -> 0 us
    all_to_all x0 -> x2, blocking collectives: none -> 67.9 us  [exchange(): lax.all_to_all(amplitudes, ('narrow', 'wide'), split_axis=0, concat_axis=...]
    all_to_all x2 -> x0, waiting for transfers between devices: 33.8 us -> none  [exchange(): lax.all_to_all(amplitudes, ('narrow', 'wide'), split_axis=0, concat_axis=...]
    all_to_all x2 -> x0, starting transfers between devices: 30.7 us -> none  [exchange(): lax.all_to_all(amplitudes, ('narrow', 'wide'), split_axis=0, concat_axis=...]
    pallas_call x3, Pallas kernels: 58.6 us -> 47.2 us  [the longest x1 20.8 us: shards(): pl.pallas_call(first_kernel, out_shape=(AMPLITUDES, HALVES, HALVES, jax.S...]
    slice x1 -> x0, local copies, waits for them, and re-layouts: 1.45 us -> none  [index_tables(): gate_orders[:, position:position + 1]]
    unnamed x10 -> x0, local copies, waits for them, and re-layouts: 1.41 us -> none
  transfers between devices with their start and end apart: 2 -> 0, of which waited for: 2 -> 0; matrix products, arithmetic and copies ran while one was open for 0% -> 0% of each run, Pallas kernels for 0% -> 0%
where the time goes in v1:
time: 119 us
  blocking collectives  67.9 us (57%)
  Pallas kernels  47.2 us (40%)
  local copies, waits for them, and re-layouts  3.57 us (3%)
    all_to_all x2, blocking collectives, exchange(): lax.all_to_all(amplitudes, ('narrow', 'wide'), split_axis=0, concat_axis=...  67.9 us
    pallas_call x1, Pallas kernels, shards(): pl.pallas_call(first_kernel, out_shape=(AMPLITUDES, HALVES, HALVES, jax.S...  20.8 us
    pallas_call x1, Pallas kernels, shards(): pl.pallas_call(third_kernel, out_shape=AMPLITUDES, in_specs=[SMEM] + [VME...  18.1 us
    pallas_call x1, Pallas kernels, shards(): pl.pallas_call(second_kernel, out_shape=AMPLITUDES, in_specs=[SMEM] + [VM...  8.24 us
    reshape x1, local copies, waits for them, and re-layouts, shards(): jnp.pad(propagator, (0, PROP_ROWS * 128 - propagator.shape[0]))  3.57 us

profile of v1, /device:TPU:1, one launch (start us, length us, event | category | flops | bytes accessed | tf_op | source)
XLA Modules:
  0.0 118.7 jit_solution(1296748529376368199)
XLA Ops:
  0.0 3.6 %pad_bitcast_fusion.flat = f32[5512,128]{1,0:T(8,128)} fusion(f32[705432]{0:T(1024)} %param.6), kind=kLoop, calls=%fused_computation | loop fusion | bytes 5643872 | tf_op jit(solution)/shard_map/reshape | solution.py:326
  3.6 20.8 %first.1 = (f32[512,128]{1,0:T(8,128)}, bf16[2304,512]{1,0:T(8,128)(2,1)}, bf16[2304,512]{1,0:T(8,128)(2,1)}, s32[24,128]{1,0:T(8,128)}, s32[16,128]{1,0:T(8,128)}) custom-call(s32[6,11]{1,0:T(8,128)} %orders.5, s32[24]{0:T(128)} %levels.1, s32[16,128]{1,0:T(8,128)} %bitcast.18, f32[512,128]{1,0:T(8,128)} %bitcast.16, f32[5512,128]{1,0:T(8,128)} %pad_bitcast_fusion.flat), custom_call_target="tpu_custom_call" | custom-call | tf_op jit(solution)/shard_map/first/pallas_call | solution.py:327
  24.4 39.8 %all_to_all.22 = f32[512,1,128]{2,1,0:T(1,128)} all-to-all(f32[512,1,128]{2,1,0:T(1,128)} %bitcast.17), channel_id=1, replica_groups=mesh['wide'=64,'narrow'=8] {'narrow','wide'}, dimensions={0} | all-to-all | bytes 524288 | tf_op jit(solution)/shard_map/all_to_all | solution.py:322
  64.1 8.2 %second.1 = f32[512,128]{1,0:T(8,128)} custom-call(s32[6,11]{1,0:T(8,128)} %orders.5, f32[512,128]{1,0:T(8,128)} %bitcast.14, bf16[2304,512]{1,0:T(8,128)(2,1)} %get-tuple-element.11.hi, bf16[2304,512]{1,0:T(8,128)(2,1)} %get-tuple-element.12.lo, s32[24,128]{1,0:T(8,128)} %get-tuple-element.13.padded, s32[16,128]{1,0:T(8,128)} %get-tuple-element.14.places), custom_call_target="tpu_custom_call" | custom-call | tf_op jit(solution)/shard_map/second/pallas_call | solution.py:342
  72.4 28.2 %all_to_all.23 = f32[512,1,128]{2,1,0:T(1,128)} all-to-all(f32[512,1,128]{2,1,0:T(1,128)} %bitcast.15), channel_id=1, replica_groups=mesh['wide'=64,'narrow'=8] {'narrow','wide'}, dimensions={0} | all-to-all | bytes 524288 | tf_op jit(solution)/shard_map/all_to_all | solution.py:322
  100.5 18.1 %third.1 = f32[512,128]{1,0:T(8,128)} custom-call(s32[6,11]{1,0:T(8,128)} %orders.5, f32[512,128]{1,0:T(8,128)} %bitcast.13, bf16[2304,512]{1,0:T(8,128)(2,1)} %get-tuple-element.11.hi, bf16[2304,512]{1,0:T(8,128)(2,1)} %get-tuple-element.12.lo, s32[24,128]{1,0:T(8,128)} %get-tuple-element.13.padded, s32[16,128]{1,0:T(8,128)} %get-tuple-element.14.places), custom_call_target="tpu_custom_call" | custom-call | tf_op jit(solution)/shard_map/third/pallas_call | solution.py:351

commit v2 on v1

--- a/solution.py
+++ b/solution.py
@@ -65,32 +65,43 @@
         row0 = GROUPS[group][2]
         column = 0
         for degree in degrees:
-            n = SIZES[degree]
-            for r in range(n):
-                origin = starts[degree] + n * r - column
-                first, shift = divmod(origin, 128)
-                for i in range(2):
-                    low, high = max(column, 128 * i), min(column + n, 128 * i + 128)
-                    if low >= high:
-                        blocks[pl.ds(i * PADDED + row0 + column + r, 1), :] = jnp.zeros((1, 128), F32)
-                        continue
-                    low, high = low - 128 * i, high - 128 * i
-                    value = None
-                    if low < 128 - shift:
-                        value = flat[pl.ds(first + i, 1), :]
-                        if shift:
-                            value = pltpu.roll(value, 128 - shift, 1)
-                    if shift and high > 128 - shift:
-                        after = pltpu.roll(flat[pl.ds(first + i + 1, 1), :], 128 - shift, 1)
-                        value = (
-                            after
-                            if value is None
-                            else jnp.where(lane[:1] < 128 - shift, value, after)
-                        )
-                    if low > 0 or high < 128:
-                        value = jnp.where((lane[:1] >= low) & (lane[:1] < high), value, 0.0)
-                    blocks[pl.ds(i * PADDED + row0 + column + r, 1), :] = value
-            column += n
+            small_sector(flat, blocks, starts[degree], SIZES[degree], row0, column)
+            column += SIZES[degree]
+
+
+def small_sector(flat, blocks, start, n, row0, column):
+    lane = lax.broadcasted_iota(jnp.int32, (8, 128), 1)
+    row = lax.broadcasted_iota(jnp.int32, (8, 128), 0)
+    step, extra = divmod(n, 128)
+    sides = [i for i in range(2) if max(column, 128 * i) < min(column + n, 128 * i + 128)]
+    for r in range(0, n, 8):
+        count = min(8, n - r)
+        first, shift = divmod(start + n * r - column, 128)
+        spot = lane + (row * extra + shift)
+        from_lane = spot & 127
+        spot = lax.shift_right_logical(spot, 7)
+        last = (shift + extra * (count - 1) + 127) >> 7
+        turned = {}
+        for m in range(min(sides), max(sides) + last + 1):
+            if step:
+                at = min(first + m, PROP_ROWS - 8)
+                piece = flat[pl.ds(at, 8), :]
+            else:
+                at = min(first + m, PROP_ROWS - 1)
+                piece = jnp.broadcast_to(flat[pl.ds(at, 1), :], (8, 128))
+            turned[m] = take(piece, from_lane)
+        for i in range(2):
+            target = pl.ds(i * PADDED + row0 + column + r, count)
+            if i not in sides:
+                blocks[target, :] = jnp.zeros((count, 128), F32)
+                continue
+            value = turned[i]
+            for m in range(1, last + 1):
+                value = jnp.where(spot == m, turned[i + m], value)
+            low, high = column - 128 * i, column + n - 128 * i
+            if low > 0 or high < 128:
+                value = jnp.where((lane >= low) & (lane < high), value, 0.0)
+            blocks[target, :] = value[:count]
 
 
 def split_blocks(blocks, hi, lo):
@@ -181,44 +192,74 @@
         push[pl.ds(8 * half, 8), :] = found
 
 
-def permute(source, target, table, source_blocks, target_blocks, unroll):
+def move_block(source, target, table, source_blocks, o):
+    index = jnp.broadcast_to(table[pl.ds(o, 1), :], (8, 128))
+    block, lane = lax.shift_right_arithmetic(index, 7), index & 127
+    hits = [block == i for i in range(source_blocks)]
+    for b in range(4):
+        found = jnp.zeros((8, 128), F32)
+        for i in range(source_blocks):
+            piece = source[8 * b : 8 * b + 8, 128 * i : 128 * i + 128]
+            found = jnp.where(hits[i], take(piece, lane), found)
+        at = o * 128 if isinstance(o, int) else pl.multiple_of(o * 128, 128)
+        target[8 * b : 8 * b + 8, pl.ds(at, 128)] = found
+
+
+def multiply(u, y, hi, lo, at, k):
+    x = u[:, at : at + k]
+    xh = x.astype(BF16)
+    xl = (x - xh.astype(F32)).astype(BF16)
+    both = lax.dot_general(
+        jnp.concatenate([xh, xl], axis=0), hi[at : at + k, :k], NT, preferred_element_type=F32
+    )
+    rest = lax.dot_general(xh, lo[at : at + k, :k], NT, preferred_element_type=F32)
+    y[:, at : at + k] = both[:32] + both[32:] + rest
+
+
+def gate(orders, number, top, x, u, y, hi, lo, padded, places, pull, push, ready=None):
+    tables(orders, number, top, padded, places, pull, push)
+    for group, (_, _, at, k) in enumerate(GROUPS):
+        for o in range(at // 128, (at + k) // 128):
+            move_block(x, u, pull, BLOCKS, o)
+        if ready is not None:
+            ready(group)
+        multiply(u, y, hi, lo, at, k)
+    scatter(x, y, push)
+
+
+def scatter(x, y, push):
     def body(t, carry):
-        for step in range(unroll):
-            o = t * unroll + step
-            index = jnp.broadcast_to(table[pl.ds(o, 1), :], (8, 128))
-            block, lane = lax.shift_right_arithmetic(index, 7), index & 127
-            hits = [block == i for i in range(source_blocks)]
-            for b in range(4):
-                found = jnp.zeros((8, 128), F32)
-                for i in range(source_blocks):
-                    piece = source[8 * b : 8 * b + 8, 128 * i : 128 * i + 128]
-                    found = jnp.where(hits[i], take(piece, lane), found)
-                target[8 * b : 8 * b + 8, pl.ds(pl.multiple_of(o * 128, 128), 128)] = found
+        for step in range(8):
+            move_block(y, x, push, PADDED_BLOCKS, t * 8 + step)
         return carry
 
-    lax.fori_loop(0, target_blocks // unroll, body, 0)
-
-
-def multiply(u, y, hi, lo):
-    for _, _, at, k in GROUPS:
-        x = u[:, at : at + k]
-        xh = x.astype(BF16)
-        xl = (x - xh.astype(F32)).astype(BF16)
-        both = lax.dot_general(
-            jnp.concatenate([xh, xl], axis=0),
-            hi[at : at + k, :k],
-            NT,
-            preferred_element_type=F32,
+    lax.fori_loop(0, BLOCKS // 8, body, 0)
+
+
+def half_copies(hi_from, lo_from, hi_to, lo_to, sems):
+    copies = []
+    for group, (_, _, at, k) in enumerate(GROUPS):
+        rows = pl.ds(at, k)
+        copies.append(
+            (
+                pltpu.make_async_copy(hi_from.at[rows, :], hi_to.at[rows, :], sems.at[2 * group]),
+                pltpu.make_async_copy(lo_from.at[rows, :], lo_to.at[rows, :], sems.at[2 * group + 1]),
+            )
         )
-        rest = lax.dot_general(xh, lo[at : at + k, :k], NT, preferred_element_type=F32)
-        y[:, at : at + k] = both[:32] + both[32:] + rest
-
-
-def gate(orders, number, top, x, u, y, hi, lo, padded, places, pull, push):
-    tables(orders, number, top, padded, places, pull, push)
-    permute(x, u, pull, BLOCKS, PADDED_BLOCKS, 3)
-    multiply(u, y, hi, lo)
-    permute(y, x, push, PADDED_BLOCKS, BLOCKS, 2)
+    return copies
+
+
+def fetch(hi_hbm, lo_hbm, hi, lo, sems):
+    copies = half_copies(hi_hbm, lo_hbm, hi, lo, sems)
+    for pair in copies:
+        for copy in pair:
+            copy.start()
+
+    def ready(group):
+        for copy in copies[group]:
+            copy.wait()
+
+    return ready
 
 
 def turn_in(value, at, x):
@@ -253,8 +294,17 @@
 
 
 def first_kernel(
-    orders, levels, order, wave, flat, out, hi, lo, padded, places, blocks, x, u, y, pull, push, plain
+    orders, levels, order, wave, tail, propagator,
+    out, hi_hbm, lo_hbm, padded, places,
+    flat, blocks, hi, lo, x, u, y, pull, push, plain, flat_sem, sems,
 ):
+    length = (PROP_ROWS - 1) * 128
+    load = pltpu.make_async_copy(
+        propagator.at[pl.ds(0, length)],
+        flat.reshape(PROP_ROWS * 128).at[pl.ds(0, length)],
+        flat_sem,
+    )
+    load.start()
     device = lax.axis_index("wide") * 8 + lax.axis_index("narrow")
     high = jnp.int32(0)
     for s in range(8):
@@ -265,9 +315,6 @@
     for s in range(6):
         lane_energy = lane_energy + levels[s] * (spin(lane, s) * spin(lane, s + 1))
     last_lane_spin = spin(lane, 6)
-
-    lay_out_blocks(flat, blocks)
-    split_blocks(blocks, hi, lo)
     pad_order(order, padded)
     invert_order(padded, places)
     for at in range(0, 512, 128):
@@ -277,24 +324,41 @@
         for s in range(8):
             energy = energy + levels[7 + s] * (spins[s] * spins[s + 1])
         turn_in(wave[pl.ds(at, 128), :] * jnp.exp(-ZZ_RATE * energy.astype(F32)), at, x)
+    load.wait()
+    flat[pl.ds(PROP_ROWS - 1, 1), :] = tail[...]
+    lay_out_blocks(flat, blocks)
+    split_blocks(blocks, hi, lo)
+    saves = half_copies(hi, lo, hi_hbm, lo_hbm, sems)
+    for pair in saves:
+        for copy in pair:
+            copy.start()
     rest = (x, u, y, hi, lo, padded, places, pull, push)
     gate(orders, 0, True, *rest)
     top_out(x, plain)
     low_in(plain, x)
     gate(orders, 1, False, *rest)
     low_out(x, out)
-
-
-def second_kernel(orders, amplitudes, hi, lo, padded, places, out, x, u, y, pull, push):
+    for pair in saves:
+        for copy in pair:
+            copy.wait()
+
+
+def second_kernel(
+    orders, amplitudes, padded, places, hi_hbm, lo_hbm, out, hi, lo, x, u, y, pull, push, sems
+):
+    ready = fetch(hi_hbm, lo_hbm, hi, lo, sems)
     top_in(amplitudes, x)
-    gate(orders, 2, True, x, u, y, hi, lo, padded, places, pull, push)
+    gate(orders, 2, True, x, u, y, hi, lo, padded, places, pull, push, ready)
     top_out(x, out)
 
 
-def third_kernel(orders, amplitudes, hi, lo, padded, places, out, x, u, y, pull, push, plain):
+def third_kernel(
+    orders, amplitudes, padded, places, hi_hbm, lo_hbm, out, hi, lo, x, u, y, pull, push, plain, sems
+):
+    ready = fetch(hi_hbm, lo_hbm, hi, lo, sems)
     rest = (x, u, y, hi, lo, padded, places, pull, push)
     low_in(amplitudes, x)
-    gate(orders, 3, False, *rest)
+    gate(orders, 3, False, *rest, ready)
     low_out(x, plain)
     top_in(plain, x)
     gate(orders, 4, True, *rest)
@@ -306,9 +370,12 @@
 
 SMEM = pl.BlockSpec(memory_space=pltpu.SMEM)
 VMEM = pl.BlockSpec(memory_space=pltpu.VMEM)
+ANY = pl.BlockSpec(memory_space=pl.ANY)
 AMPLITUDES = jax.ShapeDtypeStruct((512, 128), F32)
 HALVES = jax.ShapeDtypeStruct((PADDED, 512), BF16)
 SCRATCH = [
+    pltpu.VMEM((PADDED, 512), BF16),
+    pltpu.VMEM((PADDED, 512), BF16),
     pltpu.VMEM((32, STATES), F32),
     pltpu.VMEM((32, PADDED), F32),
     pltpu.VMEM((32, PADDED), F32),
@@ -316,6 +383,7 @@
     pltpu.VMEM((16, 128), jnp.int32),
 ]
 PLAIN = pltpu.VMEM((512, 128), F32)
+SEMS = pltpu.SemaphoreType.DMA((12,))
 
 
 def exchange(amplitudes):
@@ -323,8 +391,9 @@
 
 
 def shards(wavefunction, propagator, gate_orders, sector_order, bond_level):
-    flat = jnp.pad(propagator, (0, PROP_ROWS * 128 - propagator.shape[0])).reshape(-1, 128)
-    amplitudes, *rest = pl.pallas_call(
+    length = (PROP_ROWS - 1) * 128
+    tail = jnp.pad(propagator[length:], (0, PROP_ROWS * 128 - propagator.shape[0])).reshape(1, 128)
+    amplitudes, hi, lo, padded, places = pl.pallas_call(
         first_kernel,
         out_shape=(
             AMPLITUDES,
@@ -333,29 +402,43 @@
             jax.ShapeDtypeStruct((24, 128), jnp.int32),
             jax.ShapeDtypeStruct((16, 128), jnp.int32),
         ),
-        in_specs=[SMEM, SMEM, VMEM, VMEM, VMEM],
-        out_specs=(VMEM,) * 5,
-        scratch_shapes=[pltpu.VMEM((4 * PADDED, 128), F32), *SCRATCH, PLAIN],
+        in_specs=[SMEM, SMEM, VMEM, VMEM, VMEM, ANY],
+        out_specs=(VMEM, ANY, ANY, VMEM, VMEM),
+        scratch_shapes=[
+            pltpu.VMEM((PROP_ROWS, 128), F32),
+            pltpu.VMEM((4 * PADDED, 128), F32),
+            *SCRATCH,
+            PLAIN,
+            pltpu.SemaphoreType.DMA,
+            SEMS,
+        ],
         name="first",
-    )(gate_orders, bond_level, sector_order.reshape(16, 128), wavefunction.reshape(512, 128), flat)
+    )(
+        gate_orders,
+        bond_level,
+        sector_order.reshape(16, 128),
+        wavefunction.reshape(512, 128),
+        tail,
+        propagator,
+    )
     amplitudes = exchange(amplitudes)
     amplitudes = pl.pallas_call(
         second_kernel,
         out_shape=AMPLITUDES,
-        in_specs=[SMEM] + [VMEM] * 5,
+        in_specs=[SMEM, VMEM, VMEM, VMEM, ANY, ANY],
         out_specs=VMEM,
-        scratch_shapes=SCRATCH,
+        scratch_shapes=[*SCRATCH, SEMS],
         name="second",
-    )(gate_orders, amplitudes, *rest)
+    )(gate_orders, amplitudes, padded, places, hi, lo)
     amplitudes = exchange(amplitudes)
     amplitudes = pl.pallas_call(
         third_kernel,
         out_shape=AMPLITUDES,
-        in_specs=[SMEM] + [VMEM] * 5,
+        in_specs=[SMEM, VMEM, VMEM, VMEM, ANY, ANY],
         out_specs=VMEM,
-        scratch_shapes=[*SCRATCH, PLAIN],
+        scratch_shapes=[*SCRATCH, PLAIN, SEMS],
         name="third",
-    )(gate_orders, amplitudes, *rest)
+    )(gate_orders, amplitudes, padded, places, hi, lo)
     return amplitudes.reshape(-1)
 
 

time: 119 us -> 104 us (0.87)
  Pallas kernels: 47.2 us -> 34.9 us
  local copies, waits for them, and re-layouts: 3.57 us -> 1.27 us
    pallas_call x2, Pallas kernels: 26.4 us -> 19.5 us  [the longest x1 13.1 us: shards(): pl.pallas_call(third_kernel, out_shape=AMPLITUDES, in_specs=[SMEM, VMEM,...]
    pallas_call x1, Pallas kernels: 20.8 us -> 15.4 us  [shards(): pl.pallas_call(first_kernel, out_shape=(AMPLITUDES, HALVES, HALVES, jax.S...]
    reshape x1, local copies, waits for them, and re-layouts: 3.57 us -> 0.58 us  [shards(): jnp.pad(propagator[length:], (0, PROP_ROWS * 128 - propagator.shape[0]))]
where the time goes in v2:
time: 104 us
  blocking collectives  67.7 us (65%)
  Pallas kernels  34.9 us (34%)
  local copies, waits for them, and re-layouts  1.27 us (1%)
    all_to_all x2, blocking collectives, exchange(): lax.all_to_all(amplitudes, ('narrow', 'wide'), split_axis=0, concat_axis=...  67.7 us
    pallas_call x1, Pallas kernels, shards(): pl.pallas_call(first_kernel, out_shape=(AMPLITUDES, HALVES, HALVES, jax.S...  15.4 us
    pallas_call x1, Pallas kernels, shards(): pl.pallas_call(third_kernel, out_shape=AMPLITUDES, in_specs=[SMEM, VMEM,...  13.1 us
    pallas_call x1, Pallas kernels, shards(): pl.pallas_call(second_kernel, out_shape=AMPLITUDES, in_specs=[SMEM, VMEM,...  6.47 us

profile of v2, /device:TPU:1, one launch (start us, length us, event | category | flops | bytes accessed | tf_op | source)
XLA Modules:
  0.0 104.1 jit_solution(8544873171431569218)
XLA Ops:
  0.0 0.7 slice.3
  0.7 0.6 pad_bitcast_fusion.tail
  1.3 15.4 %first.1 = (f32[512,128]{1,0:T(8,128)}, bf16[2304,512]{1,0:T(8,128)(2,1)}, bf16[2304,512]{1,0:T(8,128)(2,1)}, s32[24,128]{1,0:T(8,128)}, s32[16,128]{1,0:T(8,128)}) custom-call(s32[6,11]{1,0:T(8,128)} %orders.5, s32[24]{0:T(128)} %levels.1, s32[16,128]{1,0:T(8,128)} %bitcast.18, f32[512,128]{1,0:T(8,128)} %bitcast.17, f32[1,128]{1,0:T(1,128)} %pad_bitcast_fusion.tail, ...), custom_call_target="tpu_custom_call" | custom-call | tf_op jit(solution)/shard_map/first/pallas_call | solution.py:396
  16.7 39.8 %all_to_all.22 = f32[512,1,128]{2,1,0:T(1,128)} all-to-all(f32[512,1,128]{2,1,0:T(1,128)} %bitcast.16), channel_id=1, replica_groups=mesh['wide'=64,'narrow'=8] {'narrow','wide'}, dimensions={0} | all-to-all | bytes 524288 | tf_op jit(solution)/shard_map/all_to_all | solution.py:390
  56.5 6.5 %second.1 = f32[512,128]{1,0:T(8,128)} custom-call(s32[6,11]{1,0:T(8,128)} %orders.5, f32[512,128]{1,0:T(8,128)} %bitcast.14, s32[24,128]{1,0:T(8,128)} %get-tuple-element.11.padded, s32[16,128]{1,0:T(8,128)} %get-tuple-element.12.places, bf16[2304,512]{1,0:T(8,128)(2,1)} %get-tuple-element.13.hi_hbm, bf16[2304,512]{1,0:T(8,128)(2,1)} %get-tuple-element.14.lo_hbm), custom_call_target="tpu_custom_call" | custom-call | tf_op jit(solution)/shard_map/second/pallas_call | solution.py:425
  62.9 27.9 %all_to_all.23 = f32[512,1,128]{2,1,0:T(1,128)} all-to-all(f32[512,1,128]{2,1,0:T(1,128)} %bitcast.15), channel_id=1, replica_groups=mesh['wide'=64,'narrow'=8] {'narrow','wide'}, dimensions={0} | all-to-all | bytes 524288 | tf_op jit(solution)/shard_map/all_to_all | solution.py:390
  90.9 13.1 %third.1 = f32[512,128]{1,0:T(8,128)} custom-call(s32[6,11]{1,0:T(8,128)} %orders.5, f32[512,128]{1,0:T(8,128)} %bitcast.13, s32[24,128]{1,0:T(8,128)} %get-tuple-element.11.padded, s32[16,128]{1,0:T(8,128)} %get-tuple-element.12.places, bf16[2304,512]{1,0:T(8,128)(2,1)} %get-tuple-element.13.hi_hbm, bf16[2304,512]{1,0:T(8,128)(2,1)} %get-tuple-element.14.lo_hbm), custom_call_target="tpu_custom_call" | custom-call | tf_op jit(solution)/shard_map/third/pallas_call | solution.py:434

commit v3 on v2

--- a/solution.py
+++ b/solution.py
@@ -53,6 +53,7 @@
         row0 = GROUPS[group][2]
         columns = -(-n // 128)
         step = n // 2
+        placed = row0
         for s in range(64):
             count = len(range(s, n, 64))
             first, shift = divmod(starts[degree] + n * s, 128)
@@ -60,7 +61,8 @@
                 lambda i: flat[pl.ds(first + i, count, stride=step), :], count, shift, columns
             )
             for i in range(columns):
-                blocks[pl.ds(i * PADDED + row0 + s, count, stride=64), :] = rows[i]
+                blocks[pl.ds(i * PADDED + placed, count), :] = rows[i]
+            placed += count
     for group, degrees in ((0, (0, 1, 2, 3)), (5, (8, 9, 10, 11))):
         row0 = GROUPS[group][2]
         column = 0
@@ -146,6 +148,15 @@
     for o in range(PADDED_BLOCKS):
         state = padded[pl.ds(o, 1), :]
         place = lane + 128 * o
+        for _, n, at, k in GROUPS[1:5]:
+            if at <= 128 * o < at + k:
+                row_of_block = place - at
+                fewest, more = divmod(n, 64)
+                slot = row_of_block & 63
+                place = (
+                    at + slot * fewest + jnp.minimum(slot, more)
+                    + lax.shift_right_logical(row_of_block, 6)
+                )
         hit = lax.shift_right_arithmetic(state, 7) == row
         left = jnp.concatenate(
             [
@@ -216,8 +227,7 @@
     y[:, at : at + k] = both[:32] + both[32:] + rest
 
 
-def gate(orders, number, top, x, u, y, hi, lo, padded, places, pull, push, ready=None):
-    tables(orders, number, top, padded, places, pull, push)
+def gate(x, u, y, hi, lo, pull, push, ready=None):
     for group, (_, _, at, k) in enumerate(GROUPS):
         for o in range(at // 128, (at + k) // 128):
             move_block(x, u, pull, BLOCKS, o)
@@ -236,30 +246,20 @@
     lax.fori_loop(0, BLOCKS // 8, body, 0)
 
 
-def half_copies(hi_from, lo_from, hi_to, lo_to, sems):
-    copies = []
-    for group, (_, _, at, k) in enumerate(GROUPS):
-        rows = pl.ds(at, k)
-        copies.append(
-            (
-                pltpu.make_async_copy(hi_from.at[rows, :], hi_to.at[rows, :], sems.at[2 * group]),
-                pltpu.make_async_copy(lo_from.at[rows, :], lo_to.at[rows, :], sems.at[2 * group + 1]),
-            )
+def copies_by_group(source, target, sems):
+    return [
+        pltpu.make_async_copy(
+            source.at[pl.ds(at, k), :], target.at[pl.ds(at, k), :], sems.at[group]
         )
-    return copies
-
-
-def fetch(hi_hbm, lo_hbm, hi, lo, sems):
-    copies = half_copies(hi_hbm, lo_hbm, hi, lo, sems)
-    for pair in copies:
-        for copy in pair:
-            copy.start()
-
-    def ready(group):
-        for copy in copies[group]:
-            copy.wait()
-
-    return ready
+        for group, (_, _, at, k) in enumerate(GROUPS)
+    ]
+
+
+def fetch(lo_hbm, lo, sems):
+    copies = copies_by_group(lo_hbm, lo, sems)
+    for copy in copies:
+        copy.start()
+    return lambda group: copies[group].wait()
 
 
 def turn_in(value, at, x):
@@ -294,96 +294,112 @@
 
 
 def first_kernel(
-    orders, levels, order, wave, tail, propagator,
-    out, hi_hbm, lo_hbm, padded, places,
-    flat, blocks, hi, lo, x, u, y, pull, push, plain, flat_sem, sems,
+    orders, levels, order_hbm, wave_hbm, tail, propagator,
+    out, hi, lo_hbm, padded, places,
+    flat, blocks, order, wave, lo, x, u, y, pull, push, plain, in_sems, sems,
 ):
     length = (PROP_ROWS - 1) * 128
     load = pltpu.make_async_copy(
         propagator.at[pl.ds(0, length)],
         flat.reshape(PROP_ROWS * 128).at[pl.ds(0, length)],
-        flat_sem,
+        in_sems.at[0],
     )
     load.start()
+    order_load = pltpu.make_async_copy(order_hbm, order, in_sems.at[1])
+    order_load.start()
+    wave_load = pltpu.make_async_copy(wave_hbm, wave, in_sems.at[2])
+    wave_load.start()
     device = lax.axis_index("wide") * 8 + lax.axis_index("narrow")
     high = jnp.int32(0)
     for s in range(8):
         high = high + levels[LB + s] * spin(device, s) * spin(device, s + 1)
     border = levels[LB - 1] * spin(device, 0)
-    lane = lax.broadcasted_iota(jnp.int32, (128, 128), 1)
-    lane_energy = jnp.zeros((128, 128), jnp.int32) + high
-    for s in range(6):
-        lane_energy = lane_energy + levels[s] * (spin(lane, s) * spin(lane, s + 1))
-    last_lane_spin = spin(lane, 6)
+    lane = lax.broadcasted_iota(jnp.int32, (8, 128), 1)
+    row = lax.broadcasted_iota(jnp.int32, (8, 128), 0)
+    spins = [spin(lane, t) for t in range(7)] + [spin(row, t) for t in range(3)]
+    common = jnp.zeros((8, 128), jnp.int32) + high
+    for t in range(9):
+        common = common + levels[t] * (spins[t] * spins[t + 1])
+    joined = {z: common + (z * levels[9]) * spins[9] for z in (1, -1)}
+    order_load.wait()
     pad_order(order, padded)
     invert_order(padded, places)
+    wave_load.wait()
     for at in range(0, 512, 128):
-        row = lax.broadcasted_iota(jnp.int32, (128, 128), 0) + at
-        spins = [spin(row, s) for s in range(9)]
-        energy = lane_energy + levels[6] * (last_lane_spin * spins[0]) + border * spins[8]
-        for s in range(8):
-            energy = energy + levels[7 + s] * (spins[s] * spins[s + 1])
-        turn_in(wave[pl.ds(at, 128), :] * jnp.exp(-ZZ_RATE * energy.astype(F32)), at, x)
+        pieces = []
+        for block in range(at // 8, at // 8 + 16):
+            z = [1 - 2 * (block >> t & 1) for t in range(6)]
+            rest = border * z[5]
+            for t in range(5):
+                rest = rest + levels[10 + t] * (z[t] * z[t + 1])
+            energy = joined[z[0]] + rest
+            pieces.append(
+                wave[pl.ds(8 * block, 8), :] * jnp.exp(-ZZ_RATE * energy.astype(F32))
+            )
+        turn_in(jnp.concatenate(pieces, axis=0), at, x)
     load.wait()
     flat[pl.ds(PROP_ROWS - 1, 1), :] = tail[...]
     lay_out_blocks(flat, blocks)
     split_blocks(blocks, hi, lo)
-    saves = half_copies(hi, lo, hi_hbm, lo_hbm, sems)
-    for pair in saves:
-        for copy in pair:
-            copy.start()
-    rest = (x, u, y, hi, lo, padded, places, pull, push)
-    gate(orders, 0, True, *rest)
+    saves = copies_by_group(lo, lo_hbm, sems)
+    for copy in saves:
+        copy.start()
+    rest = (x, u, y, hi, lo, pull, push)
+    tables(orders, 0, True, padded, places, pull, push)
+    gate(*rest)
     top_out(x, plain)
     low_in(plain, x)
-    gate(orders, 1, False, *rest)
+    tables(orders, 1, False, padded, places, pull, push)
+    gate(*rest)
     low_out(x, out)
-    for pair in saves:
-        for copy in pair:
-            copy.wait()
-
-
-def second_kernel(
-    orders, amplitudes, padded, places, hi_hbm, lo_hbm, out, hi, lo, x, u, y, pull, push, sems
-):
-    ready = fetch(hi_hbm, lo_hbm, hi, lo, sems)
+    for copy in saves:
+        copy.wait()
+
+
+def tables_kernel(orders, padded, places, pull, push):
+    for i, number in enumerate((2, 3, 4, 5)):
+        tables(orders, number, number in (2, 4), padded, places, pull.at[i], push.at[i])
+
+
+def second_kernel(amplitudes, pull, push, hi, lo_hbm, out, lo, x, u, y, sems):
+    ready = fetch(lo_hbm, lo, sems)
     top_in(amplitudes, x)
-    gate(orders, 2, True, x, u, y, hi, lo, padded, places, pull, push, ready)
+    gate(x, u, y, hi, lo, pull.at[0], push.at[0], ready)
     top_out(x, out)
 
 
-def third_kernel(
-    orders, amplitudes, padded, places, hi_hbm, lo_hbm, out, hi, lo, x, u, y, pull, push, plain, sems
-):
-    ready = fetch(hi_hbm, lo_hbm, hi, lo, sems)
-    rest = (x, u, y, hi, lo, padded, places, pull, push)
+def third_kernel(amplitudes, pull, push, hi, lo_hbm, out, lo, x, u, y, plain, sems):
+    ready = fetch(lo_hbm, lo, sems)
     low_in(amplitudes, x)
-    gate(orders, 3, False, *rest, ready)
+    gate(x, u, y, hi, lo, pull.at[1], push.at[1], ready)
     low_out(x, plain)
     top_in(plain, x)
-    gate(orders, 4, True, *rest)
+    gate(x, u, y, hi, lo, pull.at[2], push.at[2])
     top_out(x, plain)
     low_in(plain, x)
-    gate(orders, 5, False, *rest)
+    gate(x, u, y, hi, lo, pull.at[3], push.at[3])
     low_out(x, out)
 
 
 SMEM = pl.BlockSpec(memory_space=pltpu.SMEM)
 VMEM = pl.BlockSpec(memory_space=pltpu.VMEM)
-ANY = pl.BlockSpec(memory_space=pl.ANY)
+HBM = pl.BlockSpec(memory_space=pltpu.HBM)
 AMPLITUDES = jax.ShapeDtypeStruct((512, 128), F32)
-HALVES = jax.ShapeDtypeStruct((PADDED, 512), BF16)
+HALF = pltpu.VMEM((PADDED, 512), BF16)
+GRANT = pltpu.CompilerParams(vmem_limit_bytes=24 << 20)
 SCRATCH = [
-    pltpu.VMEM((PADDED, 512), BF16),
-    pltpu.VMEM((PADDED, 512), BF16),
+    HALF,
     pltpu.VMEM((32, STATES), F32),
     pltpu.VMEM((32, PADDED), F32),
     pltpu.VMEM((32, PADDED), F32),
-    pltpu.VMEM((24, 128), jnp.int32),
-    pltpu.VMEM((16, 128), jnp.int32),
 ]
+TABLES = [pltpu.VMEM((24, 128), jnp.int32), pltpu.VMEM((16, 128), jnp.int32)]
 PLAIN = pltpu.VMEM((512, 128), F32)
-SEMS = pltpu.SemaphoreType.DMA((12,))
+SEMS = pltpu.SemaphoreType.DMA((6,))
+
+
+def in_hbm(array):
+    return pltpu.with_memory_space_constraint(array, pltpu.HBM)
 
 
 def exchange(amplitudes):
@@ -392,53 +408,72 @@
 
 def shards(wavefunction, propagator, gate_orders, sector_order, bond_level):
     length = (PROP_ROWS - 1) * 128
-    tail = jnp.pad(propagator[length:], (0, PROP_ROWS * 128 - propagator.shape[0])).reshape(1, 128)
+    spare = PROP_ROWS * 128 - propagator.shape[0]
+    tail = lax.pad(propagator, jnp.float32(0), [(-length, spare, 0)]).reshape(1, 128)
     amplitudes, hi, lo, padded, places = pl.pallas_call(
         first_kernel,
         out_shape=(
             AMPLITUDES,
-            HALVES,
-            HALVES,
+            HALF,
+            pltpu.HBM((PADDED, 512), BF16),
             jax.ShapeDtypeStruct((24, 128), jnp.int32),
             jax.ShapeDtypeStruct((16, 128), jnp.int32),
         ),
-        in_specs=[SMEM, SMEM, VMEM, VMEM, VMEM, ANY],
-        out_specs=(VMEM, ANY, ANY, VMEM, VMEM),
+        in_specs=[SMEM, SMEM, HBM, HBM, VMEM, HBM],
+        out_specs=(VMEM, VMEM, HBM, VMEM, VMEM),
         scratch_shapes=[
             pltpu.VMEM((PROP_ROWS, 128), F32),
             pltpu.VMEM((4 * PADDED, 128), F32),
+            pltpu.VMEM((16, 128), jnp.int32),
+            PLAIN,
             *SCRATCH,
+            *TABLES,
             PLAIN,
-            pltpu.SemaphoreType.DMA,
+            pltpu.SemaphoreType.DMA((3,)),
             SEMS,
         ],
+        compiler_params=GRANT,
         name="first",
     )(
         gate_orders,
         bond_level,
-        sector_order.reshape(16, 128),
-        wavefunction.reshape(512, 128),
+        in_hbm(sector_order.reshape(16, 128)),
+        in_hbm(wavefunction.reshape(512, 128)),
         tail,
-        propagator,
+        in_hbm(propagator),
     )
+    lo = in_hbm(lo)
     amplitudes = exchange(amplitudes)
+    pull, push = pl.pallas_call(
+        tables_kernel,
+        out_shape=(
+            jax.ShapeDtypeStruct((4, 24, 128), jnp.int32),
+            jax.ShapeDtypeStruct((4, 16, 128), jnp.int32),
+        ),
+        in_specs=[SMEM, VMEM, VMEM],
+        out_specs=(VMEM, VMEM),
+        compiler_params=GRANT,
+        name="tables",
+    )(gate_orders, padded, places)
     amplitudes = pl.pallas_call(
         second_kernel,
         out_shape=AMPLITUDES,
-        in_specs=[SMEM, VMEM, VMEM, VMEM, ANY, ANY],
+        in_specs=[VMEM, VMEM, VMEM, VMEM, HBM],
         out_specs=VMEM,
         scratch_shapes=[*SCRATCH, SEMS],
+        compiler_params=GRANT,
         name="second",
-    )(gate_orders, amplitudes, padded, places, hi, lo)
+    )(amplitudes, pull, push, hi, lo)
     amplitudes = exchange(amplitudes)
     amplitudes = pl.pallas_call(
         third_kernel,
         out_shape=AMPLITUDES,
-        in_specs=[SMEM, VMEM, VMEM, VMEM, ANY, ANY],
+        in_specs=[VMEM, VMEM, VMEM, VMEM, HBM],
         out_specs=VMEM,
         scratch_shapes=[*SCRATCH, PLAIN, SEMS],
+        compiler_params=GRANT,
         name="third",
-    )(gate_orders, amplitudes, padded, places, hi, lo)
+    )(amplitudes, pull, push, hi, lo)
     return amplitudes.reshape(-1)
 
 

time: 104 us -> 97.1 us (0.934)
  blocking collectives: 67.7 us -> 26.2 us
  starting transfers between devices: 0 us -> 22.2 us
  waiting for transfers between devices: 0 us -> 16.3 us
  Pallas kernels: 34.9 us -> 31.2 us
    all_to_all x2 -> x1, blocking collectives: 67.7 us -> 26.2 us  [exchange(): lax.all_to_all(amplitudes, ('narrow', 'wide'), split_axis=0, concat_axis=...]
    all_to_all x0 -> x1, starting transfers between devices: none -> 22.2 us  [exchange(): lax.all_to_all(amplitudes, ('narrow', 'wide'), split_axis=0, concat_axis=...]
    all_to_all x0 -> x1, waiting for transfers between devices: none -> 16.3 us  [exchange(): lax.all_to_all(amplitudes, ('narrow', 'wide'), split_axis=0, concat_axis=...]
    pallas_call x3 -> x4, Pallas kernels: 34.9 us -> 31.2 us  [the longest x1 13.7 us: shards(): pl.pallas_call(first_kernel, out_shape=(AMPLITUDES, HALF, pltpu.HBM((PADD...]
  transfers between devices with their start and end apart: 0 -> 1, of which waited for: 0 -> 1; matrix products, arithmetic and copies ran while one was open for 0% -> 0% of each run, Pallas kernels for 0% -> 1%
where the time goes in v3:
time: 97.1 us; the launch traced here: 96.8 us
  Pallas kernels  31.2 us (32%)
  blocking collectives  26.2 us (27%)
  starting transfers between devices  22.2 us (23%)
  waiting for transfers between devices  16.3 us (17%)
    all_to_all x1, blocking collectives, exchange(): lax.all_to_all(amplitudes, ('narrow', 'wide'), split_axis=0, concat_axis=...  26.2 us
    all_to_all x1, starting transfers between devices, exchange(): lax.all_to_all(amplitudes, ('narrow', 'wide'), split_axis=0, concat_axis=...  22.2 us
    all_to_all x1, waiting for transfers between devices, exchange(): lax.all_to_all(amplitudes, ('narrow', 'wide'), split_axis=0, concat_axis=...  16.3 us
    pallas_call x1, Pallas kernels, shards(): pl.pallas_call(first_kernel, out_shape=(AMPLITUDES, HALF, pltpu.HBM((PADD...  13.7 us
    pallas_call x1, Pallas kernels, shards(): pl.pallas_call(third_kernel, out_shape=AMPLITUDES, in_specs=[VMEM, VMEM,...  12 us
    pallas_call x1, Pallas kernels, shards(): pl.pallas_call(second_kernel, out_shape=AMPLITUDES, in_specs=[VMEM, VMEM,...  4.65 us
  transfers between devices with their start and end apart: 1, of which 1 were waited for; matrix products, arithmetic and copies ran while one was open for 0% of the time, Pallas kernels for 1%

profile of v3, /device:TPU:1, one launch (start us, length us, event | category | flops | bytes accessed | tf_op | source)
XLA Modules:
  0.0 96.8 jit_solution(4006212329300997382)
XLA Ops:
  0.0 0.0 copy-start
  0.0 0.0 copy-start.1
  0.0 0.7 fusion.tail
  0.7 0.0 copy-done
  0.7 0.0 copy-done.1
  0.7 13.7 %first.1 = (f32[512,128]{1,0:T(8,128)}, bf16[2304,512]{1,0:T(8,128)(2,1)S(1)}, bf16[2304,512]{1,0:T(8,128)(2,1)}, s32[24,128]{1,0:T(8,128)S(1)}, s32[16,128]{1,0:T(8,128)S(1)}) custom-call(s32[6,11]{1,0:T(8,128)S(1)} %copy-done, s32[24]{0:T(128)S(1)} %copy-done.1, s32[16,128]{1,0:T(8,128)} %bitcast.17, f32[512,128]{1,0:T(8,128)} %bitcast.16, ...), custom_call_target="tpu_custom_call" | custom-call | tf_op jit(solution)/shard_map/first/pallas_call | solution.py:413
  14.5 22.2 %all-to-all-start = ((f32[512,1,128]{2,1,0:T(1,128)}), f32[512,1,128]{2,1,0:T(1,128)S(1)}, u32[]{:S(2)}, u32[]{:S(2)}) async-start(f32[512,1,128]{2,1,0:T(1,128)} %bitcast.4), calls=%async_computation | async-start | bytes 524288 | tf_op jit(solution)/shard_map/all_to_all | solution.py:406
  36.6 0.8 tables.1
  37.5 16.3 %all-to-all-done = f32[512,1,128]{2,1,0:T(1,128)S(1)} async-done(((f32[512,1,128]{2,1,0:T(1,128)}), f32[512,1,128]{2,1,0:T(1,128)S(1)}, u32[]{:S(2)}, u32[]{:S(2)}) %all-to-all-start) | async-done | bytes 262176 | tf_op jit(solution)/shard_map/all_to_all | solution.py:406
  53.8 4.7 %second.1 = f32[512,128]{1,0:T(8,128)S(1)} custom-call(f32[512,128]{1,0:T(8,128)S(1)} %bitcast.13, s32[4,24,128]{2,1,0:T(8,128)S(1)} %get-tuple-element.15.pull, s32[4,16,128]{2,1,0:T(8,128)S(1)} %get-tuple-element.16.push, bf16[2304,512]{1,0:T(8,128)(2,1)S(1)} %get-tuple-element.17.hi, bf16[2304,512]{1,0:T(8,128)(2,1)} %get-tuple-element.18.lo_hbm), custom_call_target="tpu_custom_call" | custom-call | tf_op jit(solution)/shard_map/second/pallas_call | solution.py:458
  58.4 26.2 %all_to_all.22 = f32[512,1,128]{2,1,0:T(1,128)S(1)} all-to-all(f32[512,1,128]{2,1,0:T(1,128)S(1)} %bitcast.15), channel_id=1, replica_groups=mesh['wide'=64,'narrow'=8] {'narrow','wide'}, dimensions={0} | all-to-all | bytes 524288 | tf_op jit(solution)/shard_map/all_to_all | solution.py:406
  84.6 12.0 %third.1 = f32[512,128]{1,0:T(8,128)} custom-call(f32[512,128]{1,0:T(8,128)S(1)} %bitcast.14, s32[4,24,128]{2,1,0:T(8,128)S(1)} %get-tuple-element.15.pull, s32[4,16,128]{2,1,0:T(8,128)S(1)} %get-tuple-element.16.push, bf16[2304,512]{1,0:T(8,128)(2,1)S(1)} %get-tuple-element.17.hi, bf16[2304,512]{1,0:T(8,128)(2,1)} %get-tuple-element.18.lo_hbm), custom_call_target="tpu_custom_call" | custom-call | tf_op jit(solution)/shard_map/third/pallas_call | solution.py:468
Async XLA Ops:
  0.0 0.7 copy-start
  0.0 0.7 copy-start.1
  14.5 39.3 %all-to-all-start = ((f32[512,1,128]{2,1,0:T(1,128)}), f32[512,1,128]{2,1,0:T(1,128)S(1)}, u32[]{:S(2)}, u32[]{:S(2)}) async-start(f32[512,1,128]{2,1,0:T(1,128)} %bitcast.4), calls=%async_computation | async-start | bytes 524288 | tf_op jit(solution)/shard_map/all_to_all | solution.py:406

commit v4 on v3

--- a/solution.py
+++ b/solution.py
@@ -227,12 +227,10 @@
     y[:, at : at + k] = both[:32] + both[32:] + rest
 
 
-def gate(x, u, y, hi, lo, pull, push, ready=None):
-    for group, (_, _, at, k) in enumerate(GROUPS):
+def gate(x, u, y, hi, lo, pull, push):
+    for _, _, at, k in GROUPS:
         for o in range(at // 128, (at + k) // 128):
             move_block(x, u, pull, BLOCKS, o)
-        if ready is not None:
-            ready(group)
         multiply(u, y, hi, lo, at, k)
     scatter(x, y, push)
 
@@ -246,22 +244,6 @@
     lax.fori_loop(0, BLOCKS // 8, body, 0)
 
 
-def copies_by_group(source, target, sems):
-    return [
-        pltpu.make_async_copy(
-            source.at[pl.ds(at, k), :], target.at[pl.ds(at, k), :], sems.at[group]
-        )
-        for group, (_, _, at, k) in enumerate(GROUPS)
-    ]
-
-
-def fetch(lo_hbm, lo, sems):
-    copies = copies_by_group(lo_hbm, lo, sems)
-    for copy in copies:
-        copy.start()
-    return lambda group: copies[group].wait()
-
-
 def turn_in(value, at, x):
     turned = value.T
     for g in range(4):
@@ -295,8 +277,8 @@
 
 def first_kernel(
     orders, levels, order_hbm, wave_hbm, tail, propagator,
-    out, hi, lo_hbm, padded, places,
-    flat, blocks, order, wave, lo, x, u, y, pull, push, plain, in_sems, sems,
+    out, hi, lo, pulls, pushes,
+    flat, blocks, order, wave, padded, places, x, u, y, pull, push, plain, in_sems,
 ):
     length = (PROP_ROWS - 1) * 128
     load = pltpu.make_async_copy(
@@ -341,9 +323,6 @@
     flat[pl.ds(PROP_ROWS - 1, 1), :] = tail[...]
     lay_out_blocks(flat, blocks)
     split_blocks(blocks, hi, lo)
-    saves = copies_by_group(lo, lo_hbm, sems)
-    for copy in saves:
-        copy.start()
     rest = (x, u, y, hi, lo, pull, push)
     tables(orders, 0, True, padded, places, pull, push)
     gate(*rest)
@@ -352,26 +331,19 @@
     tables(orders, 1, False, padded, places, pull, push)
     gate(*rest)
     low_out(x, out)
-    for copy in saves:
-        copy.wait()
-
-
-def tables_kernel(orders, padded, places, pull, push):
     for i, number in enumerate((2, 3, 4, 5)):
-        tables(orders, number, number in (2, 4), padded, places, pull.at[i], push.at[i])
-
-
-def second_kernel(amplitudes, pull, push, hi, lo_hbm, out, lo, x, u, y, sems):
-    ready = fetch(lo_hbm, lo, sems)
+        tables(orders, number, number in (2, 4), padded, places, pulls.at[i], pushes.at[i])
+
+
+def second_kernel(amplitudes, pull, push, hi, lo, out, x, u, y):
     top_in(amplitudes, x)
-    gate(x, u, y, hi, lo, pull.at[0], push.at[0], ready)
+    gate(x, u, y, hi, lo, pull.at[0], push.at[0])
     top_out(x, out)
 
 
-def third_kernel(amplitudes, pull, push, hi, lo_hbm, out, lo, x, u, y, plain, sems):
-    ready = fetch(lo_hbm, lo, sems)
+def third_kernel(amplitudes, pull, push, hi, lo, out, x, u, y, plain):
     low_in(amplitudes, x)
-    gate(x, u, y, hi, lo, pull.at[1], push.at[1], ready)
+    gate(x, u, y, hi, lo, pull.at[1], push.at[1])
     low_out(x, plain)
     top_in(plain, x)
     gate(x, u, y, hi, lo, pull.at[2], push.at[2])
@@ -388,14 +360,12 @@
 HALF = pltpu.VMEM((PADDED, 512), BF16)
 GRANT = pltpu.CompilerParams(vmem_limit_bytes=24 << 20)
 SCRATCH = [
-    HALF,
     pltpu.VMEM((32, STATES), F32),
     pltpu.VMEM((32, PADDED), F32),
     pltpu.VMEM((32, PADDED), F32),
 ]
 TABLES = [pltpu.VMEM((24, 128), jnp.int32), pltpu.VMEM((16, 128), jnp.int32)]
 PLAIN = pltpu.VMEM((512, 128), F32)
-SEMS = pltpu.SemaphoreType.DMA((6,))
 
 
 def in_hbm(array):
@@ -410,27 +380,28 @@
     length = (PROP_ROWS - 1) * 128
     spare = PROP_ROWS * 128 - propagator.shape[0]
     tail = lax.pad(propagator, jnp.float32(0), [(-length, spare, 0)]).reshape(1, 128)
-    amplitudes, hi, lo, padded, places = pl.pallas_call(
+    amplitudes, hi, lo, pull, push = pl.pallas_call(
         first_kernel,
         out_shape=(
             AMPLITUDES,
             HALF,
-            pltpu.HBM((PADDED, 512), BF16),
-            jax.ShapeDtypeStruct((24, 128), jnp.int32),
-            jax.ShapeDtypeStruct((16, 128), jnp.int32),
+            HALF,
+            jax.ShapeDtypeStruct((4, 24, 128), jnp.int32),
+            jax.ShapeDtypeStruct((4, 16, 128), jnp.int32),
         ),
         in_specs=[SMEM, SMEM, HBM, HBM, VMEM, HBM],
-        out_specs=(VMEM, VMEM, HBM, VMEM, VMEM),
+        out_specs=(VMEM,) * 5,
         scratch_shapes=[
             pltpu.VMEM((PROP_ROWS, 128), F32),
             pltpu.VMEM((4 * PADDED, 128), F32),
             pltpu.VMEM((16, 128), jnp.int32),
             PLAIN,
+            pltpu.VMEM((24, 128), jnp.int32),
+            pltpu.VMEM((16, 128), jnp.int32),
             *SCRATCH,
             *TABLES,
             PLAIN,
             pltpu.SemaphoreType.DMA((3,)),
-            SEMS,
         ],
         compiler_params=GRANT,
         name="first",
@@ -442,25 +413,13 @@
         tail,
         in_hbm(propagator),
     )
-    lo = in_hbm(lo)
     amplitudes = exchange(amplitudes)
-    pull, push = pl.pallas_call(
-        tables_kernel,
-        out_shape=(
-            jax.ShapeDtypeStruct((4, 24, 128), jnp.int32),
-            jax.ShapeDtypeStruct((4, 16, 128), jnp.int32),
-        ),
-        in_specs=[SMEM, VMEM, VMEM],
-        out_specs=(VMEM, VMEM),
-        compiler_params=GRANT,
-        name="tables",
-    )(gate_orders, padded, places)
     amplitudes = pl.pallas_call(
         second_kernel,
         out_shape=AMPLITUDES,
-        in_specs=[VMEM, VMEM, VMEM, VMEM, HBM],
+        in_specs=[VMEM] * 5,
         out_specs=VMEM,
-        scratch_shapes=[*SCRATCH, SEMS],
+        scratch_shapes=SCRATCH,
         compiler_params=GRANT,
         name="second",
     )(amplitudes, pull, push, hi, lo)
@@ -468,9 +427,9 @@
     amplitudes = pl.pallas_call(
         third_kernel,
         out_shape=AMPLITUDES,
-        in_specs=[VMEM, VMEM, VMEM, VMEM, HBM],
+        in_specs=[VMEM] * 5,
         out_specs=VMEM,
-        scratch_shapes=[*SCRATCH, PLAIN, SEMS],
+        scratch_shapes=[*SCRATCH, PLAIN],
         compiler_params=GRANT,
         name="third",
     )(amplitudes, pull, push, hi, lo)

time: 97.1 us -> 93.4 us (0.962)
  blocking collectives: 26.2 us -> 65.4 us
  starting transfers between devices: 22.2 us -> 0 us
  waiting for transfers between devices: 16.3 us -> 0 us
  Pallas kernels: 31.2 us -> 27.1 us
    all_to_all x1 -> x2, blocking collectives: 26.2 us -> 65.4 us  [exchange(): lax.all_to_all(amplitudes, ('narrow', 'wide'), split_axis=0, concat_axis=...]
    all_to_all x1 -> x0, starting transfers between devices: 22.2 us -> none  [exchange(): lax.all_to_all(amplitudes, ('narrow', 'wide'), split_axis=0, concat_axis=...]
    all_to_all x1 -> x0, waiting for transfers between devices: 16.3 us -> none  [exchange(): lax.all_to_all(amplitudes, ('narrow', 'wide'), split_axis=0, concat_axis=...]
    pallas_call x4 -> x3, Pallas kernels: 31.2 us -> 27.1 us  [the longest x1 13.1 us: shards(): pl.pallas_call(first_kernel, out_shape=(AMPLITUDES, HALF, HALF, jax.Shape...]
  transfers between devices with their start and end apart: 1 -> 0, of which waited for: 1 -> 0; matrix products, arithmetic and copies ran while one was open for 0% -> 0% of each run, Pallas kernels for 1% -> 0%
where the time goes in v4:
time: 93.4 us; the launch traced here: 93.2 us
  blocking collectives  65.4 us (70%)
  Pallas kernels  27.1 us (29%)
    all_to_all x2, blocking collectives, exchange(): lax.all_to_all(amplitudes, ('narrow', 'wide'), split_axis=0, concat_axis=...  65.4 us
    pallas_call x1, Pallas kernels, shards(): pl.pallas_call(first_kernel, out_shape=(AMPLITUDES, HALF, HALF, jax.Shape...  13.1 us
    pallas_call x1, Pallas kernels, shards(): pl.pallas_call(third_kernel, out_shape=AMPLITUDES, in_specs=[VMEM] * 5, o...  10.5 us
    pallas_call x1, Pallas kernels, shards(): pl.pallas_call(second_kernel, out_shape=AMPLITUDES, in_specs=[VMEM] * 5,...  3.36 us

profile of v4, /device:TPU:1, one launch (start us, length us, event | category | flops | bytes accessed | tf_op | source)
XLA Modules:
  0.0 93.2 jit_solution(17045147694388783418)
XLA Ops:
  0.0 0.0 copy-start.1
  0.0 0.0 copy-start
  0.0 0.7 fusion.tail
  0.7 0.0 copy-done.1
  0.7 0.0 copy-done
  0.7 13.1 %first.1 = (f32[512,128]{1,0:T(8,128)S(1)}, bf16[2304,512]{1,0:T(8,128)(2,1)S(1)}, bf16[2304,512]{1,0:T(8,128)(2,1)S(1)}, s32[4,24,128]{2,1,0:T(8,128)S(1)}, s32[4,16,128]{2,1,0:T(8,128)S(1)}) custom-call(s32[6,11]{1,0:T(8,128)S(1)} %copy-done, s32[24]{0:T(128)S(1)} %copy-done.1, s32[16,128]{1,0:T(8,128)} %bitcast.18, f32[512,128]{1,0:T(8,128)} %bitcast.17, ...), custom_call_target="tpu_custom_call" | custom-call | tf_op jit(solution)/shard_map/first/pallas_call | solution.py:383
  13.9 39.2 %all_to_all.22 = f32[512,1,128]{2,1,0:T(1,128)S(1)} all-to-all(f32[512,1,128]{2,1,0:T(1,128)S(1)} %bitcast.16), channel_id=1, replica_groups=mesh['wide'=64,'narrow'=8] {'narrow','wide'}, dimensions={0} | all-to-all | bytes 524288 | tf_op jit(solution)/shard_map/all_to_all | solution.py:376
  53.1 3.4 %second.1 = f32[512,128]{1,0:T(8,128)S(1)} custom-call(f32[512,128]{1,0:T(8,128)S(1)} %bitcast.14, s32[4,24,128]{2,1,0:T(8,128)S(1)} %get-tuple-element.11.pull, s32[4,16,128]{2,1,0:T(8,128)S(1)} %get-tuple-element.12.push, bf16[2304,512]{1,0:T(8,128)(2,1)S(1)} %get-tuple-element.13.hi, bf16[2304,512]{1,0:T(8,128)(2,1)S(1)} %get-tuple-element.14.lo), custom_call_target="tpu_custom_call" | custom-call | tf_op jit(solution)/shard_map/second/pallas_call | solution.py:417
  56.4 26.2 %all_to_all.23 = f32[512,1,128]{2,1,0:T(1,128)S(1)} all-to-all(f32[512,1,128]{2,1,0:T(1,128)S(1)} %bitcast.15), channel_id=1, replica_groups=mesh['wide'=64,'narrow'=8] {'narrow','wide'}, dimensions={0} | all-to-all | bytes 524288 | tf_op jit(solution)/shard_map/all_to_all | solution.py:376
  82.6 10.5 %third.1 = f32[512,128]{1,0:T(8,128)} custom-call(f32[512,128]{1,0:T(8,128)S(1)} %bitcast.13, s32[4,24,128]{2,1,0:T(8,128)S(1)} %get-tuple-element.11.pull, s32[4,16,128]{2,1,0:T(8,128)S(1)} %get-tuple-element.12.push, bf16[2304,512]{1,0:T(8,128)(2,1)S(1)} %get-tuple-element.13.hi, bf16[2304,512]{1,0:T(8,128)(2,1)S(1)} %get-tuple-element.14.lo), custom_call_target="tpu_custom_call" | custom-call | tf_op jit(solution)/shard_map/third/pallas_call | solution.py:427
Async XLA Ops:
  0.0 0.7 copy-start.1
  0.0 0.7 copy-start

commit v5 on v4

--- a/solution.py
+++ b/solution.py
@@ -236,12 +236,8 @@
 
 
 def scatter(x, y, push):
-    def body(t, carry):
-        for step in range(8):
-            move_block(y, x, push, PADDED_BLOCKS, t * 8 + step)
-        return carry
-
-    lax.fori_loop(0, BLOCKS // 8, body, 0)
+    for o in range(BLOCKS):
+        move_block(y, x, push, PADDED_BLOCKS, o)
 
 
 def turn_in(value, at, x):

time: 93.4 us -> 92 us (0.985)
  Pallas kernels: 27.1 us -> 25.8 us
where the time goes in v5:
time: 92 us; the launch traced here: 91.8 us
  blocking collectives  65.2 us (71%)
  Pallas kernels  25.8 us (28%)
    all_to_all x2, blocking collectives, exchange(): lax.all_to_all(amplitudes, ('narrow', 'wide'), split_axis=0, concat_axis=...  65.2 us
    pallas_call x1, Pallas kernels, shards(): pl.pallas_call(first_kernel, out_shape=(AMPLITUDES, HALF, HALF, jax.Shape...  12.7 us
    pallas_call x1, Pallas kernels, shards(): pl.pallas_call(third_kernel, out_shape=AMPLITUDES, in_specs=[VMEM] * 5, o...  9.95 us
    pallas_call x1, Pallas kernels, shards(): pl.pallas_call(second_kernel, out_shape=AMPLITUDES, in_specs=[VMEM] * 5,...  3.2 us

profile of v5, /device:TPU:1, one launch (start us, length us, event | category | flops | bytes accessed | tf_op | source)
XLA Modules:
  0.0 91.8 jit_solution(12232996851032289446)
XLA Ops:
  0.0 0.0 copy-start.1
  0.0 0.0 copy-start
  0.0 0.7 fusion.tail
  0.7 0.0 copy-done.1
  0.7 0.0 copy-done
  0.7 12.7 %first.1 = (f32[512,128]{1,0:T(8,128)S(1)}, bf16[2304,512]{1,0:T(8,128)(2,1)S(1)}, bf16[2304,512]{1,0:T(8,128)(2,1)S(1)}, s32[4,24,128]{2,1,0:T(8,128)S(1)}, s32[4,16,128]{2,1,0:T(8,128)S(1)}) custom-call(s32[6,11]{1,0:T(8,128)S(1)} %copy-done, s32[24]{0:T(128)S(1)} %copy-done.1, s32[16,128]{1,0:T(8,128)} %bitcast.18, f32[512,128]{1,0:T(8,128)} %bitcast.17, ...), custom_call_target="tpu_custom_call" | custom-call | tf_op jit(solution)/shard_map/first/pallas_call | solution.py:379
  13.4 39.2 %all_to_all.22 = f32[512,1,128]{2,1,0:T(1,128)S(1)} all-to-all(f32[512,1,128]{2,1,0:T(1,128)S(1)} %bitcast.16), channel_id=1, replica_groups=mesh['wide'=64,'narrow'=8] {'narrow','wide'}, dimensions={0} | all-to-all | bytes 524288 | tf_op jit(solution)/shard_map/all_to_all | solution.py:372
  52.6 3.2 %second.1 = f32[512,128]{1,0:T(8,128)S(1)} custom-call(f32[512,128]{1,0:T(8,128)S(1)} %bitcast.14, s32[4,24,128]{2,1,0:T(8,128)S(1)} %get-tuple-element.11.pull, s32[4,16,128]{2,1,0:T(8,128)S(1)} %get-tuple-element.12.push, bf16[2304,512]{1,0:T(8,128)(2,1)S(1)} %get-tuple-element.13.hi, bf16[2304,512]{1,0:T(8,128)(2,1)S(1)} %get-tuple-element.14.lo), custom_call_target="tpu_custom_call" | custom-call | tf_op jit(solution)/shard_map/second/pallas_call | solution.py:413
  55.8 26.0 %all_to_all.23 = f32[512,1,128]{2,1,0:T(1,128)S(1)} all-to-all(f32[512,1,128]{2,1,0:T(1,128)S(1)} %bitcast.15), channel_id=1, replica_groups=mesh['wide'=64,'narrow'=8] {'narrow','wide'}, dimensions={0} | all-to-all | bytes 524288 | tf_op jit(solution)/shard_map/all_to_all | solution.py:372
  81.8 10.0 %third.1 = f32[512,128]{1,0:T(8,128)} custom-call(f32[512,128]{1,0:T(8,128)S(1)} %bitcast.13, s32[4,24,128]{2,1,0:T(8,128)S(1)} %get-tuple-element.11.pull, s32[4,16,128]{2,1,0:T(8,128)S(1)} %get-tuple-element.12.push, bf16[2304,512]{1,0:T(8,128)(2,1)S(1)} %get-tuple-element.13.hi, bf16[2304,512]{1,0:T(8,128)(2,1)S(1)} %get-tuple-element.14.lo), custom_call_target="tpu_custom_call" | custom-call | tf_op jit(solution)/shard_map/third/pallas_call | solution.py:423
Async XLA Ops:
  0.0 0.7 copy-start.1
  0.0 0.7 copy-start
